TPU v7x, 128 devices: a whole 4x4x4 slice. The times are simulated.
128 devices in a mesh: det: 16 (over z, x), tm: 8 (over y, core).
Axes of the slice: x: 4, y: 4, z: 4, core: 2. Of those that a mesh axis runs over, the one named last changes fastest.
Arguments:
- tod: float32 [512, 8192], P('det', 'tm'), may hold values from -6 to 6
- noise_filter: float32 [8192], replicated, may hold values from 0.05 to 1
- mode_weight: float32 [32, 512], P(None, 'det'), may hold values from -0.25 to 0.25
- mode_coupling: float32 [512, 32], P('det'), may hold values from -1 to 1
- sample_weight: float32 [512, 8192], P('det', 'tm'), may hold values from 0.02 to 0.2
- pix_row: int32 [512, 8192], P('det', 'tm'), may hold values from 0 to 127, as said below
- pix_col: int32 [512, 8192], P('det', 'tm'), may hold values from 0 to 127
- angle_bin: int32 [512, 8192], P('det', 'tm'), may hold values from 0 to 63
- tile_slot: int32 [128], P('tm'), may hold values from 0 to 1
- slot_submap: int32 [8, 2], replicated, may hold values from 0 to 7, as said below
Outputs:
- signal_map: float32 [8, 3, 128, 128], P('tm', None, 'det')
- cov_map: float32 [8, 3, 3, 128, 128], P('tm', None, None, 'det')
Inputs may be any that keep to these rules, and one draw needn't show every extreme that they name: `slot_submap`: the 2 entries of one row are distinct, and every submap appears in exactly 2 rows. `pix_row`: among the 1024 samples of one detector in one time group (aligned runs of 1024 samples), each band of 8 pixel rows starting at a multiple of 8 holds exactly 64 samples.
All inputs are finite; a program needn't handle non-finite values.
Results may differ from a plain program's by a relative error of at most 0.000075.
Values sent between devices are 32-bit elements; how exact they have to be, the bound alone decides.
A program may use at most 64 MiB of HBM per device.

v0:
```python
import math

import jax
import jax.numpy as jnp
from jax import lax
from jax.sharding import PartitionSpec as P

SUBPIX = 128
ANG_BINS = 64
SLOTS = 2


highest = lax.Precision.HIGHEST


def phase_table(left_len, right_len, modulus):
    left_index = jnp.arange(left_len, dtype=jnp.int32)
    right_index = jnp.arange(right_len, dtype=jnp.int32)
    product = left_index[:, None] * right_index[None, :] % modulus
    phase = product.astype(jnp.float32) * (2.0 * math.pi / modulus)
    return (jnp.cos(phase), jnp.sin(phase))


def noise_filtering(block, noise_filter):
    length = block.shape[2]
    count = block.shape[1]
    second_len = 128
    first_len = length // second_len
    data = block.reshape(count, first_len, second_len)
    cos_one, sin_one = phase_table(first_len, first_len, first_len)
    cos_two, sin_two = phase_table(second_len, second_len, second_len)
    turn_cos, turn_sin = phase_table(first_len, second_len, length)
    real_a = jnp.einsum("ab,rbc->rac", cos_one, data, precision=highest)
    imag_a = -jnp.einsum("ab,rbc->rac", sin_one, data, precision=highest)
    real_b = real_a * turn_cos + imag_a * turn_sin
    imag_b = imag_a * turn_cos - real_a * turn_sin
    real_c = jnp.einsum("rab,bc->rac", real_b, cos_two, precision=highest) + jnp.einsum(
        "rab,bc->rac", imag_b, sin_two, precision=highest
    )
    imag_c = jnp.einsum("rab,bc->rac", imag_b, cos_two, precision=highest) - jnp.einsum(
        "rab,bc->rac", real_b, sin_two, precision=highest
    )
    gain = noise_filter.reshape(second_len, first_len).T
    real_c = real_c * gain
    imag_c = imag_c * gain
    real_d = jnp.einsum("rab,bc->rac", real_c, cos_two, precision=highest) - jnp.einsum(
        "rab,bc->rac", imag_c, sin_two, precision=highest
    )
    imag_d = jnp.einsum("rab,bc->rac", imag_c, cos_two, precision=highest) + jnp.einsum(
        "rab,bc->rac", real_c, sin_two, precision=highest
    )
    real_e = real_d * turn_cos - imag_d * turn_sin
    imag_e = imag_d * turn_cos + real_d * turn_sin
    output = jnp.einsum("ab,rbc->rac", cos_one, real_e, precision=highest) - jnp.einsum(
        "ab,rbc->rac", sin_one, imag_e, precision=highest
    )
    return (output / length).reshape(1, count, length)


def term_stacks(weighted, sample_weight, angles):
    cosine = jnp.cos(angles)
    sine_part = jnp.sin(angles)
    row_stack = jnp.stack(
        [weighted, sample_weight, sample_weight * cosine, sample_weight * sine_part], 0
    )
    col_stack = jnp.stack([jnp.ones_like(cosine), cosine, sine_part], 0)
    return (row_stack, col_stack)


def body(
    tod,
    noise_filter,
    mode_weight,
    mode_coupling,
    sample_weight,
    pix_row,
    pix_col,
    angle_bin,
    tile_slot,
    slot_submap,
):
    groups = lax.axis_size("tm")
    my_group = lax.axis_index("tm")
    det_dev, samp_dev = tod.shape
    per_group = det_dev // groups
    stacked = tod.reshape(groups, per_group, samp_dev)
    wide = (lambda block: noise_filtering(block, noise_filter))(
        lax.all_to_all(stacked, "tm", split_axis=0, concat_axis=2, tiled=True)
    )
    weight_cols = lax.dynamic_slice_in_dim(mode_weight, my_group * per_group, per_group, 1)
    couple_rows = lax.dynamic_slice_in_dim(mode_coupling, my_group * per_group, per_group, 0)
    partial_modes = jnp.dot(
        weight_cols, wide[0], precision=highest, preferred_element_type=jnp.float32
    )
    mode_amps = lax.psum(partial_modes, ("det", "tm"))
    wide = (
        wide
        - jnp.dot(couple_rows, mode_amps, precision=highest, preferred_element_type=jnp.float32)[
            None
        ]
    )
    returned = lax.all_to_all(wide, "tm", split_axis=2, concat_axis=0, tiled=True).reshape(
        det_dev, samp_dev
    )
    row_terms = 4
    col_terms = 3
    weighted = sample_weight * returned
    tiles = tile_slot.shape[0]
    tile_size = samp_dev // tiles
    lanes = jnp.arange(SUBPIX, dtype=jnp.int32)
    angles = angle_bin.astype(jnp.float32) * (2.0 * math.pi / ANG_BINS)
    row_stack, col_stack = term_stacks(weighted, sample_weight, angles)
    pieces = 4
    piece_rows = det_dev // pieces
    initial = jnp.zeros((SLOTS, row_terms * SUBPIX, col_terms * SUBPIX), jnp.float32)

    def tile_turn(index, accum):
        start = index * tile_size
        row_part = lax.dynamic_slice_in_dim(row_stack, start, tile_size, 2)
        rows_here = lax.dynamic_slice_in_dim(pix_row, start, tile_size, 1)
        cols_here = lax.dynamic_slice_in_dim(pix_col, start, tile_size, 1)
        col_part = lax.dynamic_slice_in_dim(col_stack, start, tile_size, 2)
        term = jnp.zeros((row_terms * SUBPIX, col_terms * SUBPIX), jnp.float32)
        for piece in range(pieces):
            lower = piece * piece_rows
            upper = lower + piece_rows
            row_onehot = (rows_here[lower:upper].reshape(-1)[:, None] == lanes[None, :]).astype(
                jnp.float32
            )
            col_onehot = (cols_here[lower:upper].reshape(-1)[:, None] == lanes[None, :]).astype(
                jnp.float32
            )
            row_values = row_part[:, lower:upper].reshape(row_terms, -1).T
            samples = row_values.shape[0]
            left = (row_values[:, :, None] * row_onehot[:, None, :]).reshape(
                samples, row_terms * SUBPIX
            )
            col_values = col_part[:, lower:upper].reshape(col_terms, -1).T
            right = (col_values[:, :, None] * col_onehot[:, None, :]).reshape(
                samples, col_terms * SUBPIX
            )
            term = term + lax.dot_general(
                left,
                right,
                (((0,), (0,)), ((), ())),
                precision=highest,
                preferred_element_type=jnp.float32,
            )
        slot_here = tile_slot[index]
        current = lax.dynamic_index_in_dim(accum, slot_here, 0, keepdims=False)
        return lax.dynamic_update_index_in_dim(accum, current + term, slot_here, 0)

    accum = lax.fori_loop(0, tiles, tile_turn, initial)
    shaped = accum.reshape(SLOTS, row_terms, SUBPIX, col_terms, SUBPIX)
    reduced = lax.psum_scatter(shaped, "det", scatter_dimension=2, tiled=True)
    my_slots = slot_submap[my_group]
    submap_ids = jnp.arange(groups, dtype=jnp.int32)
    select = (submap_ids[:, None] == my_slots[None, :]).astype(jnp.float32)
    spread = jnp.tensordot(select, reduced, axes=(1, 0), precision=highest)
    owned = lax.psum_scatter(spread, "tm", scatter_dimension=0, tiled=True)
    signal = jnp.transpose(owned[:, 0], (0, 2, 1, 3))
    covariance = jnp.transpose(owned[:, 1:], (0, 1, 3, 2, 4))
    return (signal, covariance)


def solution(mesh):
    return jax.shard_map(
        body,
        mesh=mesh,
        in_specs=(
            P("det", "tm"),
            P(),
            P(None, "det"),
            P("det", None),
            P("det", "tm"),
            P("det", "tm"),
            P("det", "tm"),
            P("det", "tm"),
            P("tm"),
            P(),
        ),
        out_specs=(P("tm", None, "det", None), P("tm", None, None, "det", None)),
        check_vma=False,
    )
```

profile of v0, /device:TPU:1, one launch (start us, length us, event | category | flops | bytes accessed | tf_op | source)
XLA Modules:
  0.0 817.7 jit_solution(7961361014666019864)
XLA Ops:
  8.8 6.0 all-to-all-start
  15.8 4.2 all-to-all-done
  28.0 149.1 %all-reduce.4.cloned.1.call-done = f32[32,8192]{1,0:T(8,128)} async-done(((f32[32,8192]{1,0:T(8,128)}), f32[32,8192]{1,0:T(8,128)}) %all-reduce.4.cloned.1.call-update) | async-done | bytes 1048592 | tf_op jit(solution)/shard_map/psum | solution.py:95
  179.0 6.7 copy.50
  186.2 38.4 %reduce.2 = f32[8192,4]{1,0:T(8,128)} reduce(f32[8192,1,4]{2,1,0:T(1,128)} %bitcast.192, f32[]{:T(128)} %broadcast.373), dimensions={1}, to_apply=%bitcast.117.reduce_sub_computation | reduce | bytes 262148
  224.6 5.6 reshape.536
  230.2 3.8 all-to-all-start.1
  234.0 5.2 all-to-all-done.1
  240.2 8.7 %reshape.537 = f32[8192,1,4]{2,1,0:T(1,128)} reshape(f32[8,4096]{1,0:T(8,128)S(1)} %reduce.3) | data formatting | bytes 262144
  254.6 431.5 %while.15 = (s32[]{:T(128)}, f32[2,512,384]{2,1,0:T(8,128)}, s32[16]{0:T(128)S(1)}, f32[4,32,1024]{2,1,0:T(8,128)S(1)}, s32[32,1024]{1,0:T(8,128)}, /*index=5*/f...) while((s32[]{:T(128)}, f32[2,512,384]{2,1,0:T(8,128)}, ...), condition=%wide.region_2.3_spmd.clone.clone, body=%wide.region_1.2_spmd.clone.clone.sunk | while | flops 4835508224 | bytes 29270340 | solution.py:153
  275.3 3.4 convolution_add_fusion.7
  280.2 3.5 convolution_add_fusion.8
  288.9 4.4 fusion.210
  306.4 3.5 convolution_add_fusion.8
  315.0 4.4 fusion.210
  332.5 3.5 convolution_add_fusion.8
  341.2 4.4 fusion.210
  358.7 3.5 convolution_add_fusion.8
  367.4 4.4 fusion.210
  384.9 3.5 convolution_add_fusion.8
  393.6 4.4 fusion.210
  411.1 3.5 convolution_add_fusion.8
  419.8 4.4 fusion.210
  432.4 3.4 convolution_add_fusion.7
  437.3 3.5 convolution_add_fusion.8
  446.0 4.4 fusion.210
  463.5 3.5 convolution_add_fusion.8
  472.2 4.4 fusion.210
  489.7 3.5 convolution_add_fusion.8
  498.4 4.4 fusion.210
  515.9 3.5 convolution_add_fusion.8
  524.5 4.4 fusion.210
  537.2 3.4 convolution_add_fusion.7
  542.1 3.5 convolution_add_fusion.8
  550.7 4.4 fusion.210
  568.3 3.5 convolution_add_fusion.8
  576.9 4.4 fusion.210
  594.4 3.5 convolution_add_fusion.8
  603.1 4.4 fusion.210
  620.6 3.5 convolution_add_fusion.8
  629.3 4.4 fusion.210
  646.8 3.5 convolution_add_fusion.8
  655.5 4.4 fusion.210
  668.1 3.4 convolution_add_fusion.7
  673.1 3.5 convolution_add_fusion.8
  681.7 4.4 fusion.210
  692.9 83.7 %all-reduce.6.cloned.1.call-done = f32[2,4,128,3,128]{4,1,3,0,2:T(4,128)} async-done(((f32[2,4,128,3,128]{4,1,3,0,2:T(4,128)}), f32[2,4,128,3,128]{4,1,3,0,2:T(4,128)}) %all-reduce.6.cloned.1.call-update) | async-done | bytes 1572880
  778.7 29.6 %reduce-scatter.2.cloned.1.call-done = f32[1,4,8,3,128]{4,2,3,1,0:T(8,128)} async-done(((f32[8,4,8,3,128]{4,2,3,1,0:T(8,128)}), f32[1,4,8,3,128]{4,2,3,1,0:T(8,128)}) %reduce-scatter.2.cloned.1.call-update) | async-done | bytes 49168 | tf_op jit(solution)/shard_map/reduce_scatter | solution.py:160
  (804 shorter events, 276.1 us)
Async XLA Ops:
  7.2 18.8 %copy-start = (f32[32,32]{1,0:T(8,128)S(1)}, f32[32,32]{1,0:T(8,128)}, u32[]{:S(2)}) copy-start(f32[32,32]{1,0:T(8,128)} %param.14) | copy-start | bytes 12292
  8.8 11.2 %all-to-all-start = ((f32[8,4,1024]{2,1,0:T(4,128)}), f32[8,4,1024]{2,1,0:T(4,128)S(1)}, u32[]{:S(2)}, u32[]{:S(2)}) async-start(f32[8,4,1024]{2,1,0:T(4,128)} %reshape.505), calls=%async_computation | async-start | bytes 262144 | tf_op jit(solution)/shard_map/all_to_all | solution.py:88
  14.7 162.4 %all-reduce.4.cloned.1.call-start = ((), (), s32[]{:S(2)}) async-start(), calls=%async_computation.3 | async-start | bytes 2097152 | tf_op jit(solution)/shard_map/psum | solution.py:95
  230.2 9.1 %all-to-all-start.1 = ((f32[8,1,4096]{2,1,0:T(1,128)}), f32[8,1,4096]{2,1,0:T(1,128)S(1)}, u32[]{:S(2)}, u32[]{:S(2)}) async-start(f32[8,1,4096]{2,1,0:T(1,128)} %reshape.536), calls=%async_computation.1 | async-start | bytes 262144 | tf_op jit(solution)/shard_map/all_to_all | solution.py:102
  234.0 542.5 %all-reduce.6.cloned.1.call-start = ((), (), s32[]{:S(2)}) async-start(), calls=%async_computation.5 | async-start | bytes 3145728
  248.9 3.0 copy-start.1
  248.9 3.0 copy-start.2
  252.4 2.2 copy-start.4
  690.8 0.7 copy-start.5
  690.8 1.9 copy-start.3
  690.8 117.5 %reduce-scatter.2.cloned.1.call-start = ((), (), s32[]{:S(2)}) async-start(), calls=%async_computation.4 | async-start | bytes 442368 | tf_op jit(solution)/shard_map/reduce_scatter | solution.py:160
Sparse Core Ops, SparseCore 0:
  28.1 148.9 all-reduce.3
  690.9 85.5 all-reduce.5
  778.9 29.4 reduce-scatter.1
where the time goes:
time: 822 us; the launch traced here: 818 us
  waiting for transfers between devices  272 us (33%)
  matrix products  245 us (30%)
  local copies, waits for them, and re-layouts  134 us (16%)
  other arithmetic  95 us (12%)
  loops' own time  47.1 us (6%)
  between operations  14.8 us (2%)
  starting transfers between devices  9.84 us (1%)
    dot_general x64, matrix products, tile_turn(): lax.dot_general(left, right, (((0,), (0,)), ((), ())), precision=highest,...  235 us
    psum x1, waiting for transfers between devices, body(): mode_amps = lax.psum(partial_modes, ('det', 'tm'))  149 us
    unnamed x4, waiting for transfers between devices  83.7 us
    another operation x1, loops' own time, body(): accum = lax.fori_loop(0, tiles, tile_turn, initial)  47.1 us
    mul x64, other arithmetic, tile_turn(): row_values[:, :, None] * row_onehot[:, None, :]  45.1 us
    unnamed x1, other arithmetic  38.4 us
    reduce_scatter x1, waiting for transfers between devices, body(): owned = lax.psum_scatter(spread, 'tm', scatter_dimension=0, tiled=True)  29.6 us
    dynamic_slice x16, local copies, waits for them, and re-layouts, tile_turn(): current = lax.dynamic_index_in_dim(accum, slot_here, 0, keepdims=False)  19 us
  transfers between devices with their start and end apart: 5, of which 5 were waited for; matrix products, arithmetic and copies ran while one was open for 0% of the time, Pallas kernels for 0%

commit v1 on v0

v1 whole, which is shorter than its diff:
```python
import math

import jax
import jax.numpy as jnp
import numpy as np
from jax import lax
from jax.experimental import pallas as pl
from jax.experimental.pallas import tpu as pltpu
from jax.sharding import PartitionSpec as P

F32 = jnp.float32
BF16 = jnp.bfloat16
MESH = pl.DeviceIdType.MESH
ND = 16
NT = 8


def split_const(table):
    hi = table.astype(jnp.bfloat16)
    lo = (table - hi.astype(np.float64)).astype(jnp.bfloat16)
    return hi, lo


def dft_tables():
    one = np.arange(64)
    ang = 2.0 * math.pi * (np.outer(one, one) % 64) / 64
    first = np.concatenate([np.cos(ang), -np.sin(ang)], 0)
    lane = np.arange(128)
    k2 = 2 * (lane % 64) + lane // 64
    ang = 2.0 * math.pi * (np.outer(lane, k2) % 128) / 128
    co, si = np.cos(ang), np.sin(ang)
    second = np.block([[co, -si], [si, co]])
    third = np.block([[co.T, si.T], [-si.T, co.T]])
    ang = 2.0 * math.pi * np.outer(one, lane) / 8192
    turn = np.stack([np.cos(ang), np.sin(ang)]).astype(np.float32)
    return first, first.T / 8192.0, second, third, turn


def split(value):
    hi = value.astype(BF16)
    lo = (value - hi.astype(F32)).astype(BF16)
    return hi, lo


def mm(a, b):
    return lax.dot_general(a, b, (((1,), (0,)), ((), ())), preferred_element_type=F32)


def dot3(a, b):
    return mm(a[0], b[0]) + (mm(a[0], b[1]) + mm(a[1], b[0]))


def signal_all(me_d, me_t):
    barrier = pltpu.get_barrier_semaphore()
    for i in range(1, ND):
        pl.semaphore_signal(
            barrier, inc=1, device_id={"det": (me_d + i) % ND}, device_id_type=MESH
        )
    for i in range(1, NT):
        pl.semaphore_signal(
            barrier, inc=1, device_id={"tm": (me_t + i) % NT}, device_id_type=MESH
        )
    pl.semaphore_wait(barrier, ND - 1 + NT - 1)


def exchange(axis, size, me, src_of, dst_buf, send_sem, recv_sem):
    copies = []
    for i in range(1, size):
        peer = (me + i) % size
        copy = pltpu.make_async_remote_copy(
            src_ref=src_of(peer),
            dst_ref=dst_buf.at[me],
            send_sem=send_sem.at[peer],
            recv_sem=recv_sem.at[me],
            device_id={axis: peer},
            device_id_type=MESH,
        )
        copy.start()
        copies.append(copy)
    return copies


def arrive(axis, size, me, dst_buf, send_sem, recv_sem):
    for i in range(1, size):
        peer = (me + i) % size
        pltpu.make_async_remote_copy(
            src_ref=dst_buf.at[peer],
            dst_ref=dst_buf.at[peer],
            send_sem=send_sem.at[peer],
            recv_sem=recv_sem.at[peer],
            device_id={axis: peer},
            device_id_type=MESH,
        ).wait_recv()


def filter_kernel(
    tod,
    gain,
    weight,
    couple,
    ah,
    al,
    ih,
    il,
    bh,
    bl,
    ch,
    cl,
    turn,
    out,
    ybuf,
    rbuf,
    zbuf,
    zall,
    sbuf,
    xin,
    obuf,
    cin,
    s1,
    r1,
    s2,
    r2,
    s3,
    r3,
    s4,
    r4,
):
    me_d = lax.axis_index("det")
    me_t = lax.axis_index("tm")
    signal_all(me_d, me_t)
    wsp = split(weight[...])
    for a in range(8):
        y = dot3(wsp, split(tod[:, 128 * a : 128 * a + 128]))
        ybuf[2 * a] = y[:16]
        ybuf[2 * a + 1] = y[16:]
    copies = exchange("det", ND, me_d, lambda p: ybuf.at[p], rbuf, s1, r1)
    g = gain[...]
    gfull = jnp.concatenate([g[:, :64].T, g[:, 64:].T], axis=1)
    rbuf[me_d] = ybuf[me_d]
    arrive("det", ND, me_d, rbuf, s1, r1)
    total = rbuf[0]
    for i in range(1, ND):
        total = total + rbuf[i]
    zbuf[...] = total
    for c in copies:
        c.wait_send()
    copies = exchange("det", ND, me_d, lambda p: zbuf, zall, s2, r2)
    zall[me_d] = total
    csp = split(couple[...])
    arrive("det", ND, me_d, zall, s2, r2)
    cleaned = []
    for a in range(8):
        modes = jnp.concatenate([zall[2 * a], zall[2 * a + 1]], axis=0)
        cleaned.append(tod[:, 128 * a : 128 * a + 128] - dot3(csp, split(modes)))
    turned = jnp.stack(cleaned, axis=1)
    sbuf[...] = turned.reshape(NT, 4, 8, 128)
    for c in copies:
        c.wait_send()
    copies = exchange("tm", NT, me_t, lambda p: sbuf.at[p], xin, s3, r3)
    xin[me_t] = sbuf[me_t]
    arrive("tm", NT, me_t, xin, s3, r3)
    cols = [
        jnp.concatenate([xin[m, e] for m in range(NT)], axis=0) for e in range(4)
    ]
    x = jnp.concatenate(cols, axis=1)
    f = dot3((ah[...], al[...]), split(x))
    tc, ts = turn[0], turn[1]
    rows = []
    for e in range(4):
        re, im = f[:64, 128 * e : 128 * e + 128], f[64:, 128 * e : 128 * e + 128]
        rows.append(jnp.concatenate([re * tc + im * ts, im * tc - re * ts], axis=1))
    f = dot3(split(jnp.concatenate(rows, axis=0)), (bh[...], bl[...]))
    gg = jnp.concatenate([gfull, gfull], axis=1)
    f = f * jnp.concatenate([gg] * 4, axis=0)
    f = dot3(split(f), (ch[...], cl[...]))
    cols = []
    for e in range(4):
        re, im = f[64 * e : 64 * e + 64, :128], f[64 * e : 64 * e + 64, 128:]
        cols.append(jnp.concatenate([re * tc - im * ts, im * tc + re * ts], axis=0))
    f = dot3((ih[...], il[...]), split(jnp.concatenate(cols, axis=1)))
    for m in range(NT):
        for e in range(4):
            obuf[m, e] = f[8 * m : 8 * m + 8, 128 * e : 128 * e + 128]
    for c in copies:
        c.wait_send()
    copies = exchange("tm", NT, me_t, lambda p: obuf.at[p], cin, s4, r4)
    cin[me_t] = obuf[me_t]
    arrive("tm", NT, me_t, cin, s4, r4)
    back = cin[...].reshape(32, 8, 128)
    for a in range(8):
        out[:, 128 * a : 128 * a + 128] = back[:, a]
    for c in copies:
        c.wait_send()


def trig(ang):
    h = (ang - 32).astype(F32) * np.float32(np.pi / 64)
    x = h * h
    s = np.float32(-1 / 39916800)
    for k in (1 / 362880, -1 / 5040, 1 / 120, -1 / 6, 1.0):
        s = s * x + np.float32(k)
    s = s * h
    c = np.float32(1 / 479001600)
    for k in (-1 / 3628800, 1 / 40320, -1 / 720, 1 / 24, -1 / 2, 1.0):
        c = c * x + np.float32(k)
    return 2.0 * s * s - 1.0, -2.0 * s * c


def pairs(x):
    lane = lax.broadcasted_iota(jnp.int32, (16, 128), 1)
    u, v = x[:16], x[16:]
    ur = pltpu.roll(u, 64, 1)
    vr = pltpu.roll(v, 64, 1)
    return jnp.where(lane < 64, u, vr), jnp.where(lane < 64, ur, v)


def hist_kernel(slots, w_ref, cl_ref, row_ref, col_ref, ang_ref, out, val, mi, ni, term, lt, rt):
    for a in range(8):
        sl = slice(128 * a, 128 * a + 128)
        w = w_ref[:, sl]
        c, s = trig(ang_ref[:, sl])
        g = w * cl_ref[:, sl]
        wc = w * c
        for q, v in enumerate((w, wc, w * s, wc * c, wc * s, g, g * c, g * s)):
            hi = v.astype(BF16).astype(F32)
            for k, part in enumerate((hi, v - hi)):
                val[2 * q + k, 2 * a], val[2 * q + k, 2 * a + 1] = pairs(part)
        row = row_ref[:, sl]
        mi[2 * a], mi[2 * a + 1] = pairs((row % 64).astype(F32))
        ni[2 * a], ni[2 * a + 1] = pairs((row // 64 * 128 + col_ref[:, sl]).astype(F32))
    im = lax.broadcasted_iota(jnp.int32, (64, 128), 0).astype(F32).astype(BF16)
    it = lax.broadcasted_iota(jnp.int32, (256, 128), 0).astype(F32).astype(BF16)

    def tile(j, carry):
        for k in range(16):
            lanes = slice(128 * k, 128 * k + 128)
            mask = jnp.broadcast_to(mi[j, k : k + 1, :], (64, 128)).astype(BF16) == im
            for q in range(16):
                vb = jnp.broadcast_to(val[q, j, k : k + 1, :], (64, 128)).astype(BF16)
                lt[64 * q : 64 * q + 64, lanes] = jnp.where(mask, vb, jnp.zeros_like(vb))
            nb = jnp.broadcast_to(ni[j, k : k + 1, :], (256, 128)).astype(BF16)
            rt[:, lanes] = jnp.where(nb == it, jnp.ones_like(nb), jnp.zeros_like(nb))
        acc = lax.dot_general(
            lt[...], rt[...], (((1,), (1,)), ((), ())), preferred_element_type=F32
        ).reshape(8, 2, 64, 256)
        term[j] = acc[:, 0] + acc[:, 1]
        return carry

    lax.fori_loop(0, 16, tile, 0)
    for q in range(8):
        for h in range(2):

            def total(j, carry):
                second = slots[j].astype(F32)
                t = term[j, q, :, 128 * h : 128 * h + 128]
                return carry[0] + t * (1.0 - second), carry[1] + t * second

            zero = jnp.zeros((64, 128), F32)
            first, second = lax.fori_loop(0, 16, total, (zero, zero))
            out[0, q, 64 * h : 64 * h + 64, :] = first
            out[1, q, 64 * h : 64 * h + 64, :] = second


def reduce_kernel(sub, maps, signal, cov, rbuf, tbuf, ubuf, s1, r1, s2, r2):
    me_d = lax.axis_index("det")
    me_t = lax.axis_index("tm")
    signal_all(me_d, me_t)

    def band(p):
        return maps.at[:, :, pl.ds(pl.multiple_of(8 * p, 8), 8), :]

    copies = exchange("det", ND, me_d, band, rbuf, s1, r1)
    rbuf[me_d] = maps[:, :, pl.ds(pl.multiple_of(8 * me_d, 8), 8), :]
    arrive("det", ND, me_d, rbuf, s1, r1)
    sub0 = sub[me_t, 0]
    sub1 = sub[me_t, 1]
    for q in range(8):
        a0 = rbuf[0, 0, q]
        a1 = rbuf[0, 1, q]
        for i in range(1, ND):
            a0 = a0 + rbuf[i, 0, q]
            a1 = a1 + rbuf[i, 1, q]
        for n in range(NT):
            tbuf[n, q] = jnp.where(sub0 == n, a0, 0.0) + jnp.where(sub1 == n, a1, 0.0)
    for c in copies:
        c.wait_send()
    copies = exchange("tm", NT, me_t, lambda p: tbuf.at[p], ubuf, s2, r2)
    ubuf[me_t] = tbuf[me_t]
    arrive("tm", NT, me_t, ubuf, s2, r2)
    tot = []
    for q in range(8):
        a = ubuf[0, q]
        for i in range(1, NT):
            a = a + ubuf[i, q]
        tot.append(a)
    for q in range(3):
        signal[0, q] = tot[5 + q]
    w, wc, ws, wcc, wcs = tot[:5]
    full = ((w, wc, ws), (wc, wcc, wcs), (ws, wcs, w - wcc))
    for i in range(3):
        for j in range(3):
            cov[0, i, j] = full[i][j]
    for c in copies:
        c.wait_send()


def body(
    tod,
    noise_filter,
    mode_weight,
    mode_coupling,
    sample_weight,
    pix_row,
    pix_col,
    angle_bin,
    tile_slot,
    slot_submap,
):
    vm = pl.BlockSpec(memory_space=pltpu.VMEM)
    sm = pl.BlockSpec(memory_space=pltpu.SMEM)
    dma = pltpu.SemaphoreType.DMA
    first, last, second, third, turn = dft_tables()
    tables = [jnp.asarray(t) for m in (first, last, second, third) for t in split_const(m)]
    cleaned = pl.pallas_call(
        filter_kernel,
        out_shape=jax.ShapeDtypeStruct((32, 1024), F32),
        in_specs=[vm] * 13,
        out_specs=vm,
        scratch_shapes=[
            pltpu.VMEM((ND, 16, 128), F32),
            pltpu.VMEM((ND, 16, 128), F32),
            pltpu.VMEM((16, 128), F32),
            pltpu.VMEM((ND, 16, 128), F32),
            pltpu.VMEM((NT, 4, 8, 128), F32),
            pltpu.VMEM((NT, 4, 8, 128), F32),
            pltpu.VMEM((NT, 4, 8, 128), F32),
            pltpu.VMEM((NT, 4, 8, 128), F32),
            dma((ND,)),
            dma((ND,)),
            dma((ND,)),
            dma((ND,)),
            dma((NT,)),
            dma((NT,)),
            dma((NT,)),
            dma((NT,)),
        ],
        compiler_params=pltpu.CompilerParams(collective_id=0, has_side_effects=True),
    )(
        tod,
        noise_filter.reshape(64, 128),
        mode_weight,
        mode_coupling,
        *tables,
        jnp.asarray(turn),
    )
    maps = pl.pallas_call(
        hist_kernel,
        out_shape=jax.ShapeDtypeStruct((2, 8, 128, 128), F32),
        in_specs=[sm] + [vm] * 5,
        out_specs=vm,
        scratch_shapes=[
            pltpu.VMEM((16, 16, 16, 128), F32),
            pltpu.VMEM((16, 16, 128), F32),
            pltpu.VMEM((16, 16, 128), F32),
            pltpu.VMEM((16, 8, 64, 256), F32),
            pltpu.VMEM((1024, 2048), BF16),
            pltpu.VMEM((256, 2048), BF16),
        ],
        compiler_params=pltpu.CompilerParams(vmem_limit_bytes=56 << 20),
    )(tile_slot, sample_weight, cleaned, pix_row, pix_col, angle_bin)
    return pl.pallas_call(
        reduce_kernel,
        out_shape=(
            jax.ShapeDtypeStruct((1, 3, 8, 128), F32),
            jax.ShapeDtypeStruct((1, 3, 3, 8, 128), F32),
        ),
        in_specs=[sm, vm],
        out_specs=(vm, vm),
        scratch_shapes=[
            pltpu.VMEM((ND, 2, 8, 8, 128), F32),
            pltpu.VMEM((NT, 8, 8, 128), F32),
            pltpu.VMEM((NT, 8, 8, 128), F32),
            dma((ND,)),
            dma((ND,)),
            dma((NT,)),
            dma((NT,)),
        ],
        compiler_params=pltpu.CompilerParams(collective_id=1, has_side_effects=True),
    )(slot_submap, maps)


def solution(mesh):
    return jax.shard_map(
        body,
        mesh=mesh,
        in_specs=(
            P("det", "tm"),
            P(),
            P(None, "det"),
            P("det", None),
            P("det", "tm"),
            P("det", "tm"),
            P("det", "tm"),
            P("det", "tm"),
            P("tm"),
            P(),
        ),
        out_specs=(P("tm", None, "det", None), P("tm", None, None, "det", None)),
        check_vma=False,
    )
```

time: 822 us -> 88.5 us (0.11)
  waiting for transfers between devices: 272 us -> 0 us
  matrix products: 245 us -> 0 us
  local copies, waits for them, and re-layouts: 134 us -> 3.37 us
  other arithmetic: 95 us -> 0 us
  Pallas kernels: 0 us -> 84.2 us
  loops' own time: 47.1 us -> 0 us
  between operations: 14.8 us -> 0.66 us
  starting transfers between devices: 9.84 us -> 0 us
    dot_general x79 -> x0, matrix products: 245 us -> none  [the longest x64 235 us: tile_turn(): lax.dot_general(left, right, (((0,), (0,)), ((), ())), precision=highest,...]
    psum x1 -> x0, waiting for transfers between devices: 149 us -> none  [body(): mode_amps = lax.psum(partial_modes, ('det', 'tm'))]
    pallas_call x0 -> x3, Pallas kernels: none -> 84.2 us  [the longest x1 30.7 us: body(): pl.pallas_call(filter_kernel, out_shape=jax.ShapeDtypeStruct((32, 1024),...]
    unnamed x4 -> x0, waiting for transfers between devices: 83.7 us -> none
    mul x128 -> x0, other arithmetic: 50.7 us -> none  [the longest x64 45.1 us: tile_turn(): row_values[:, :, None] * row_onehot[:, None, :]]
    another operation x1 -> x0, loops' own time: 47.1 us -> none  [body(): accum = lax.fori_loop(0, tiles, tile_turn, initial)]
    unnamed x1 -> x0, other arithmetic: 38.4 us -> none
    reduce_scatter x1 -> x0, waiting for transfers between devices: 29.6 us -> none  [body(): owned = lax.psum_scatter(spread, 'tm', scatter_dimension=0, tiled=True)]
  transfers between devices with their start and end apart: 5 -> 0, of which waited for: 5 -> 0; matrix products, arithmetic and copies ran while one was open for 0% -> 0% of each run, Pallas kernels for 0% -> 0%
where the time goes in v1:
time: 88.5 us; the launch traced here: 88.2 us
  Pallas kernels  84.2 us (95%)
  local copies, waits for them, and re-layouts  3.37 us (4%)
    pallas_call x1, Pallas kernels, body(): pl.pallas_call(filter_kernel, out_shape=jax.ShapeDtypeStruct((32, 1024),...  30.7 us
    pallas_call x1, Pallas kernels, body(): pl.pallas_call(hist_kernel, out_shape=jax.ShapeDtypeStruct((2, 8, 128, 12...  28.7 us
    pallas_call x1, Pallas kernels, body(): pl.pallas_call(reduce_kernel, out_shape=(jax.ShapeDtypeStruct((1, 3, 8, 1...  24.8 us
    unnamed x5, local copies, waits for them, and re-layouts  3.37 us

profile of v1, /device:TPU:1, one launch (start us, length us, event | category | flops | bytes accessed | tf_op | source)
XLA Modules:
  0.0 88.2 jit_solution(11130315581443785618)
XLA Ops:
  0.6 30.7 %shard_map.194.cl_ref = f32[32,1024]{1,0:T(8,128)} custom-call(f32[32,1024]{1,0:T(8,128)} %tod.1, f32[64,128]{1,0:T(8,128)} %bitcast.1, f32[32,32]{1,0:T(8,128)} %weight.1, f32[32,32]{1,0:T(8,128)} %couple.1, bf16[128,64]{1,0:T(8,128)(2,1)} %constant.18.clone.ah, bf16[128,64]{1,0:T(8,128)(2,1)} %constant.19.clone.al, bf16[64,128]{1,0:T(8,128)(2,1)} %constant.20.clone.ih, ...), custom_call_target="tpu_custom_call" | custom-call | tf_op jit(solution)/shard_map/pallas_call | solution.py:324
  31.4 0.0 copy-start
  31.4 28.7 %shard_map.195.maps = f32[2,8,128,128]{3,2,1,0:T(8,128)} custom-call(s32[16]{0:T(128)} %slots.1, f32[32,1024]{1,0:T(8,128)} %w_ref.1, f32[32,1024]{1,0:T(8,128)} %shard_map.194.cl_ref, s32[32,1024]{1,0:T(8,128)} %row_ref.1, s32[32,1024]{1,0:T(8,128)} %col_ref.1, s32[32,1024]{1,0:T(8,128)} %ang_ref.1), custom_call_target="tpu_custom_call" | custom-call | tf_op jit(solution)/shard_map/pallas_call | solution.py:356
  60.0 0.0 copy-done
  60.0 0.7 copy.21.sub
  60.7 24.8 %shard_map.196 = (f32[1,3,8,128]{3,2,1,0:T(8,128)}, f32[1,3,3,8,128]{4,3,2,1,0:T(8,128)}) custom-call(s32[8,2]{1,0:T(8,128)} %copy.21.sub, f32[2,8,128,128]{3,2,1,0:T(8,128)} %shard_map.195.maps), custom_call_target="tpu_custom_call" | custom-call | tf_op jit(solution)/shard_map/pallas_call | solution.py:371
  85.5 1.3 %copy.24 = f32[1,3,8,128]{3,2,1,0:T(8,128)} copy(f32[1,3,8,128]{3,2,1,0:T(8,128)} %get-tuple-element.4) | data formatting | bytes 24576
  86.8 1.4 %copy.25 = f32[1,3,3,8,128]{4,3,2,1,0:T(8,128)} copy(f32[1,3,3,8,128]{4,3,2,1,0:T(8,128)} %get-tuple-element.5) | data formatting | bytes 73728
Async XLA Ops:
  31.4 28.7 %copy-start = (s32[8,2]{0,1:T(2,128)S(1)}, s32[8,2]{0,1:T(2,128)}, u32[]{:S(2)}) copy-start(s32[8,2]{0,1:T(2,128)} %param.28) | copy-start | bytes 196

commit v2 on v1

v2 whole, which is shorter than its diff:
```python
import math

import jax
import jax.numpy as jnp
import numpy as np
from jax import lax
from jax.experimental import pallas as pl
from jax.experimental.pallas import tpu as pltpu
from jax.sharding import PartitionSpec as P

F32 = jnp.float32
BF16 = jnp.bfloat16
MESH = pl.DeviceIdType.MESH
ND = 16
NT = 8
CUTS = (0, 6, 10, 16)


def split_const(table):
    hi = table.astype(jnp.bfloat16)
    lo = (table - hi.astype(np.float64)).astype(jnp.bfloat16)
    return hi, lo


def dft_tables():
    one = np.arange(64)
    ang = 2.0 * math.pi * (np.outer(one, one) % 64) / 64
    first = np.concatenate([np.cos(ang), -np.sin(ang)], 0)
    lane = np.arange(128)
    k2 = 2 * (lane % 64) + lane // 64
    ang = 2.0 * math.pi * (np.outer(lane, k2) % 128) / 128
    co, si = np.cos(ang), np.sin(ang)
    second = np.block([[co, -si], [si, co]])
    third = np.block([[co.T, si.T], [-si.T, co.T]])
    ang = 2.0 * math.pi * np.outer(one, lane) / 8192
    turn = np.stack([np.cos(ang), np.sin(ang)]).astype(np.float32)
    return first, first.T / 8192.0, second, third, turn


def split(value):
    hi = value.astype(BF16)
    lo = (value - hi.astype(F32)).astype(BF16)
    return hi, lo


def mm(a, b):
    return lax.dot_general(a, b, (((1,), (0,)), ((), ())), preferred_element_type=F32)


def dot3(a, b):
    return mm(a[0], b[0]) + (mm(a[0], b[1]) + mm(a[1], b[0]))


def greet(me_d, me_t):
    barrier = pltpu.get_barrier_semaphore()
    for i in range(1, ND):
        pl.semaphore_signal(
            barrier, inc=1, device_id={"det": (me_d + i) % ND}, device_id_type=MESH
        )
    for i in range(1, NT):
        pl.semaphore_signal(
            barrier, inc=1, device_id={"tm": (me_t + i) % NT}, device_id_type=MESH
        )
    return barrier


def send(axis, size, me, src_of, dst_buf, sems):
    copies = []
    for i in range(1, size):
        peer = (me + i) % size
        copy = pltpu.make_async_remote_copy(
            src_ref=src_of(peer),
            dst_ref=dst_buf.at[me],
            send_sem=sems.at[0, peer],
            recv_sem=sems.at[1, me],
            device_id={axis: peer},
            device_id_type=MESH,
        )
        copy.start()
        copies.append(copy)
    return copies


def arrive(axis, size, me, dst_buf, sems):
    for i in range(1, size):
        peer = (me + i) % size
        pltpu.make_async_remote_copy(
            src_ref=dst_buf.at[peer],
            dst_ref=dst_buf.at[peer],
            send_sem=sems.at[0, peer],
            recv_sem=sems.at[1, peer],
            device_id={axis: peer},
            device_id_type=MESH,
        ).wait_recv()


def trig(ang):
    h = (ang - 32).astype(F32) * np.float32(np.pi / 64)
    x = h * h
    s = np.float32(-1 / 39916800)
    for k in (1 / 362880, -1 / 5040, 1 / 120, -1 / 6, 1.0):
        s = s * x + np.float32(k)
    s = s * h
    c = np.float32(1 / 479001600)
    for k in (-1 / 3628800, 1 / 40320, -1 / 720, 1 / 24, -1 / 2, 1.0):
        c = c * x + np.float32(k)
    return 2.0 * s * s - 1.0, -2.0 * s * c


def pairs(x):
    lane = lax.broadcasted_iota(jnp.int32, (16, 128), 1)
    u, v = x[:16], x[16:]
    ur = pltpu.roll(u, 64, 1)
    vr = pltpu.roll(v, 64, 1)
    return jnp.where(lane < 64, u, vr), jnp.where(lane < 64, ur, v)


def put(val, a, values):
    for q, v in enumerate(values):
        hi = v.astype(BF16).astype(F32)
        for k, part in enumerate((hi, v - hi)):
            val[2 * q + k, 2 * a], val[2 * q + k, 2 * a + 1] = pairs(part)


def tile_sum(j, count, val, mi, lt, rt, term):
    im = lax.broadcasted_iota(jnp.int32, (64, 128), 0).astype(F32).astype(BF16)
    for k in range(16):
        mask = jnp.broadcast_to(mi[j, k : k + 1, :], (64, 128)).astype(BF16) == im
        for q in range(2 * count):
            vb = jnp.broadcast_to(val[q, j, k : k + 1, :], (64, 128)).astype(BF16)
            lt[k, 64 * q : 64 * q + 64, :] = jnp.where(mask, vb, jnp.zeros_like(vb))
    left = jnp.concatenate([lt[k] for k in range(16)], axis=1)
    right = jnp.concatenate([rt[j, k] for k in range(16)], axis=1)
    acc = lax.dot_general(
        left, right, (((1,), (1,)), ((), ())), preferred_element_type=F32
    ).reshape(count, 2, 64, 256)
    term[j] = acc[:, 0] + acc[:, 1]


def columns(j, ni, rt):
    it = lax.broadcasted_iota(jnp.int32, (256, 128), 0).astype(F32).astype(BF16)
    for k in range(16):
        nb = jnp.broadcast_to(ni[j, k : k + 1, :], (256, 128)).astype(BF16)
        rt[j, k] = jnp.where(nb == it, jnp.ones_like(nb), jnp.zeros_like(nb))


def by_slot(slots, term, count, maps):
    marks = [slots[j].astype(F32) for j in range(16)]
    for h in range(2):

        def one(q, carry):
            every = jnp.zeros((64, 128), F32)
            second = jnp.zeros((64, 128), F32)
            for j in range(16):
                t = term[j, q, :, 128 * h : 128 * h + 128]
                every = every + t
                second = second + t * marks[j]
            first = every - second
            for b in range(8):
                maps[8 * h + b, 0, q] = first[8 * b : 8 * b + 8]
                maps[8 * h + b, 1, q] = second[8 * b : 8 * b + 8]
            return carry

        lax.fori_loop(0, count, one, 0)


def spread(sub0, sub1, count, got, out):
    for q in range(count):
        a0 = got[0, 0, q]
        a1 = got[0, 1, q]
        for i in range(1, ND):
            a0 = a0 + got[i, 0, q]
            a1 = a1 + got[i, 1, q]
        for n in range(NT):
            out[n, q] = jnp.where(sub0 == n, a0, 0.0) + jnp.where(sub1 == n, a1, 0.0)


def noise_filtering(x, g, ah, al, bh, bl, ch, cl, ih, il, turn):
    count = x.shape[1] // 128
    tc, ts = turn[0], turn[1]
    f = dot3((ah[...], al[...]), split(x))
    rows = []
    for e in range(count):
        re, im = f[:64, 128 * e : 128 * e + 128], f[64:, 128 * e : 128 * e + 128]
        rows.append(jnp.concatenate([re * tc + im * ts, im * tc - re * ts], axis=1))
    f = dot3(split(jnp.concatenate(rows, axis=0)), (bh[...], bl[...]))
    gg = jnp.concatenate([g, g], axis=1)
    f = f * jnp.concatenate([gg] * count, axis=0)
    f = dot3(split(f), (ch[...], cl[...]))
    cols = []
    for e in range(count):
        re, im = f[64 * e : 64 * e + 64, :128], f[64 * e : 64 * e + 64, 128:]
        cols.append(jnp.concatenate([re * tc - im * ts, im * tc + re * ts], axis=0))
    return dot3((ih[...], il[...]), split(jnp.concatenate(cols, axis=1)))


def fused_kernel(
    slots,
    sub,
    tod,
    gain,
    weight,
    couple,
    w_ref,
    row_ref,
    col_ref,
    ang_ref,
    ah,
    al,
    ih,
    il,
    bh,
    bl,
    ch,
    cl,
    turn,
    out,
    ybuf,
    yin,
    sbuf,
    xin,
    zbuf,
    zin,
    fbuf,
    fin,
    ftmp,
    obuf,
    cin,
    wcs,
    valc,
    vals,
    mi,
    ni,
    ltc,
    lts,
    rt,
    termc,
    terms,
    mapc,
    maps,
    rsc,
    rss,
    tbc,
    tbs,
    ubc,
    ubs,
    sy,
    sx,
    sz,
    sf,
    so,
    sc,
    ss,
    tc_sem,
    ts_sem,
):
    me_d = lax.axis_index("det")
    me_t = lax.axis_index("tm")
    barrier = greet(me_d, me_t)
    wsp = split(weight[...])
    for a in range(8):
        x = tod[:, 128 * a : 128 * a + 128]
        ybuf[:, a, :] = dot3(wsp, split(x))
        sbuf[:, a, :] = x
    pl.semaphore_wait(barrier, ND - 1 + NT - 1)
    copies = send("det", ND, me_d, lambda p: ybuf.at[pl.ds(2 * p, 2)], yin, sy)
    copies += send("tm", NT, me_t, lambda p: sbuf.at[pl.ds(4 * p, 4)], xin, sx)
    yin[me_d] = ybuf[pl.ds(2 * me_d, 2)]
    xin[me_t] = sbuf[pl.ds(4 * me_t, 4)]
    g = gain[...]
    gfull = jnp.concatenate([g[:, :64].T, g[:, 64:].T], axis=1)
    for a in range(8):
        sl = slice(128 * a, 128 * a + 128)
        w = w_ref[:, sl]
        c, s = trig(ang_ref[:, sl])
        wc = w * c
        ws = w * s
        wcs[0, a] = wc
        wcs[1, a] = ws
        put(valc, a, (w, wc, ws, wc * c, wc * s))
        row = row_ref[:, sl]
        mi[2 * a], mi[2 * a + 1] = pairs((row % 64).astype(F32))
        ni[2 * a], ni[2 * a + 1] = pairs((row // 64 * 128 + col_ref[:, sl]).astype(F32))

    def cov_tile(j, carry):
        columns(j, ni, rt)
        tile_sum(j, 5, valc, mi, ltc, rt, termc)
        return carry

    lax.fori_loop(CUTS[0], CUTS[1], cov_tile, 0)
    arrive("det", ND, me_d, yin, sy)
    z = yin[0]
    for i in range(1, ND):
        z = z + yin[i]
    zbuf[...] = z
    copies += send("tm", NT, me_t, lambda p: zbuf, zin, sz)
    zin[me_t] = z
    lax.fori_loop(CUTS[1], CUTS[2], cov_tile, 0)
    arrive("tm", NT, me_t, xin, sx)
    arrive("tm", NT, me_t, zin, sz)
    cols = [jnp.concatenate([xin[m, e] for m in range(NT)], axis=0) for e in range(4)]
    cols += [jnp.concatenate([zin[m, e] for m in range(NT)], axis=0) for e in range(2)]
    f = noise_filtering(
        jnp.concatenate(cols, axis=1), gfull, ah, al, bh, bl, ch, cl, ih, il, turn
    )
    for m in range(NT):
        for e in range(4):
            obuf[m, e] = f[8 * m : 8 * m + 8, 128 * e : 128 * e + 128]
        for e in range(2):
            ftmp[m, e] = f[8 * m : 8 * m + 8, 512 + 128 * e : 640 + 128 * e]
    mine = ftmp[me_t]
    fbuf[...] = mine
    copies += send("det", ND, me_d, lambda p: fbuf, fin, sf)
    copies += send("tm", NT, me_t, lambda p: obuf.at[p], cin, so)
    fin[me_d] = mine
    cin[me_t] = obuf[me_t]
    lax.fori_loop(CUTS[2], CUTS[3], cov_tile, 0)
    by_slot(slots, termc, 5, mapc)
    copies += send("det", ND, me_d, lambda p: mapc.at[p], rsc, sc)
    rsc[me_d] = mapc[me_d]
    arrive("det", ND, me_d, fin, sf)
    arrive("tm", NT, me_t, cin, so)
    csp = split(couple[...])
    for a in range(8):
        modes = fin[:, :, a, :].reshape(32, 128)
        clean = cin[:, :, a, :].reshape(32, 128) - dot3(csp, split(modes))
        w = w_ref[:, 128 * a : 128 * a + 128]
        put(vals, a, (w * clean, wcs[0, a] * clean, wcs[1, a] * clean))

    def signal_tile(j, carry):
        tile_sum(j, 3, vals, mi, lts, rt, terms)
        return carry

    lax.fori_loop(0, 16, signal_tile, 0)
    by_slot(slots, terms, 3, maps)
    copies += send("det", ND, me_d, lambda p: maps.at[p], rss, ss)
    rss[me_d] = maps[me_d]
    sub0 = sub[me_t, 0]
    sub1 = sub[me_t, 1]
    arrive("det", ND, me_d, rsc, sc)
    spread(sub0, sub1, 5, rsc, tbc)
    copies += send("tm", NT, me_t, lambda p: tbc.at[p], ubc, tc_sem)
    ubc[me_t] = tbc[me_t]
    arrive("det", ND, me_d, rss, ss)
    spread(sub0, sub1, 3, rss, tbs)
    copies += send("tm", NT, me_t, lambda p: tbs.at[p], ubs, ts_sem)
    ubs[me_t] = tbs[me_t]
    arrive("tm", NT, me_t, ubc, tc_sem)
    total = ubc[0]
    for i in range(1, NT):
        total = total + ubc[i]
    out[:5] = total
    arrive("tm", NT, me_t, ubs, ts_sem)
    total = ubs[0]
    for i in range(1, NT):
        total = total + ubs[i]
    out[5:] = total
    for c in copies:
        c.wait_send()


def finish_kernel(tot, signal, cov):
    for q in range(3):
        signal[0, q] = tot[5 + q]
    w, wc, ws, wcc, wcs = (tot[q] for q in range(5))
    full = ((w, wc, ws), (wc, wcc, wcs), (ws, wcs, w - wcc))
    for i in range(3):
        for j in range(3):
            cov[0, i, j] = full[i][j]


def body(
    tod,
    noise_filter,
    mode_weight,
    mode_coupling,
    sample_weight,
    pix_row,
    pix_col,
    angle_bin,
    tile_slot,
    slot_submap,
):
    vm = pl.BlockSpec(memory_space=pltpu.VMEM)
    sm = pl.BlockSpec(memory_space=pltpu.SMEM)
    first, last, second, third, turn = dft_tables()
    ah, al = split_const(first)
    ih, il = split_const(last)
    bh, bl = split_const(second)
    ch, cl = split_const(third)
    tables = [jnp.asarray(t) for t in (ah, al, ih, il, bh, bl, ch, cl, turn)]

    def vmem(*shape, dtype=F32):
        return pltpu.VMEM(shape, dtype)

    def sems(size):
        return pltpu.SemaphoreType.DMA((2, size))

    tot = pl.pallas_call(
        fused_kernel,
        out_shape=jax.ShapeDtypeStruct((8, 8, 128), F32),
        in_specs=[sm, sm] + [vm] * 17,
        out_specs=vm,
        scratch_shapes=[
            vmem(32, 8, 128),
            vmem(ND, 2, 8, 128),
            vmem(32, 8, 128),
            vmem(NT, 4, 8, 128),
            vmem(2, 8, 128),
            vmem(NT, 2, 8, 128),
            vmem(2, 8, 128),
            vmem(ND, 2, 8, 128),
            vmem(NT, 2, 8, 128),
            vmem(NT, 4, 8, 128),
            vmem(NT, 4, 8, 128),
            vmem(2, 8, 32, 128),
            vmem(10, 16, 16, 128),
            vmem(6, 16, 16, 128),
            vmem(16, 16, 128),
            vmem(16, 16, 128),
            vmem(16, 640, 128, dtype=BF16),
            vmem(16, 384, 128, dtype=BF16),
            vmem(16, 16, 256, 128, dtype=BF16),
            vmem(16, 5, 64, 256),
            vmem(16, 3, 64, 256),
            vmem(ND, 2, 5, 8, 128),
            vmem(ND, 2, 3, 8, 128),
            vmem(ND, 2, 5, 8, 128),
            vmem(ND, 2, 3, 8, 128),
            vmem(NT, 5, 8, 128),
            vmem(NT, 3, 8, 128),
            vmem(NT, 5, 8, 128),
            vmem(NT, 3, 8, 128),
            sems(ND),
            sems(NT),
            sems(NT),
            sems(ND),
            sems(NT),
            sems(ND),
            sems(ND),
            sems(NT),
            sems(NT),
        ],
        compiler_params=pltpu.CompilerParams(
            collective_id=0, has_side_effects=True, vmem_limit_bytes=56 << 20
        ),
    )(
        tile_slot,
        slot_submap,
        tod,
        noise_filter.reshape(64, 128),
        mode_weight,
        mode_coupling,
        sample_weight,
        pix_row,
        pix_col,
        angle_bin,
        *tables,
    )
    return pl.pallas_call(
        finish_kernel,
        out_shape=(
            jax.ShapeDtypeStruct((1, 3, 8, 128), F32),
            jax.ShapeDtypeStruct((1, 3, 3, 8, 128), F32),
        ),
        in_specs=[vm],
        out_specs=(vm, vm),
    )(tot)


def solution(mesh):
    return jax.shard_map(
        body,
        mesh=mesh,
        in_specs=(
            P("det", "tm"),
            P(),
            P(None, "det"),
            P("det", None),
            P("det", "tm"),
            P("det", "tm"),
            P("det", "tm"),
            P("det", "tm"),
            P("tm"),
            P(),
        ),
        out_specs=(P("tm", None, "det", None), P("tm", None, None, "det", None)),
        check_vma=False,
    )
```

time: 88.5 us -> 56.3 us (0.64)
  Pallas kernels: 84.2 us -> 54.1 us
  local copies, waits for them, and re-layouts: 3.37 us -> 1.34 us
    pallas_call x3 -> x2, Pallas kernels: 84.2 us -> 54.1 us  [the longest x1 52.7 us: body(): pl.pallas_call(fused_kernel, out_shape=jax.ShapeDtypeStruct((8, 8, 128),...]
    unnamed x5 -> x3, local copies, waits for them, and re-layouts: 3.37 us -> 1.34 us
where the time goes in v2:
time: 56.3 us; the launch traced here: 56 us
  Pallas kernels  54.1 us (96%)
  local copies, waits for them, and re-layouts  1.34 us (2%)
  between operations  0.65 us (1%)
    pallas_call x1, Pallas kernels, body(): pl.pallas_call(fused_kernel, out_shape=jax.ShapeDtypeStruct((8, 8, 128),...  52.7 us
    pallas_call x1, Pallas kernels, body(): pl.pallas_call(finish_kernel, out_shape=(jax.ShapeDtypeStruct((1, 3, 8, 1...  1.38 us
    unnamed x3, local copies, waits for them, and re-layouts  1.34 us

profile of v2, /device:TPU:1, one launch (start us, length us, event | category | flops | bytes accessed | tf_op | source)
XLA Modules:
  0.0 56.0 jit_solution(6826743154334055483)
XLA Ops:
  0.6 0.0 copy-start
  0.6 0.7 %copy-done = s32[8,2]{0,1:T(2,128)S(1)} copy-done((s32[8,2]{0,1:T(2,128)S(1)}, s32[8,2]{0,1:T(2,128)}, u32[]{:S(2)}) %copy-start) | copy-done | bytes 88
  1.3 0.7 %copy.21.sub = s32[8,2]{1,0:T(8,128)} copy(s32[8,2]{0,1:T(2,128)S(1)} %copy-done) | data formatting | bytes 128 | tf_op args[9]
  2.0 52.7 %shard_map.194.tot = f32[8,8,128]{2,1,0:T(8,128)} custom-call(s32[16]{0:T(128)} %slots.1, s32[8,2]{1,0:T(8,128)} %copy.21.sub, f32[32,1024]{1,0:T(8,128)} %tod.1, f32[64,128]{1,0:T(8,128)} %bitcast.1, f32[32,32]{1,0:T(8,128)} %weight.1, f32[32,32]{1,0:T(8,128)} %couple.1, f32[32,1024]{1,0:T(8,128)} %w_ref.1, s32[32,1024]{1,0:T(8,128)} %row_ref.1, ...), custom_call_target="tpu_custom_call" | custom-call | tf_op jit(solution)/shard_map/pallas_call | solution.py:399
  54.7 1.4 %shard_map.195 = (f32[1,3,8,128]{3,2,1,0:T(8,128)}, f32[1,3,3,8,128]{4,3,2,1,0:T(8,128)}) custom-call(f32[8,8,128]{2,1,0:T(8,128)} %shard_map.194.tot), custom_call_target="tpu_custom_call" | custom-call | tf_op jit(solution)/shard_map/pallas_call | solution.py:460
Async XLA Ops:
  0.6 0.7 %copy-start = (s32[8,2]{0,1:T(2,128)S(1)}, s32[8,2]{0,1:T(2,128)}, u32[]{:S(2)}) copy-start(s32[8,2]{0,1:T(2,128)} %param.28) | copy-start | bytes 196

commit v3 on v2

--- a/solution.py
+++ b/solution.py
@@ -13,7 +13,9 @@
 MESH = pl.DeviceIdType.MESH
 ND = 16
 NT = 8
-CUTS = (0, 6, 10, 16)
+GROUP = 8
+CUTS = (0, 1, 4)
+STEPS = (0, 4, 8)
 
 
 def split_const(table):
@@ -95,7 +97,7 @@
 
 
 def trig(ang):
-    h = (ang - 32).astype(F32) * np.float32(np.pi / 64)
+    h = (ang - 32.0) * np.float32(np.pi / 64)
     x = h * h
     s = np.float32(-1 / 39916800)
     for k in (1 / 362880, -1 / 5040, 1 / 120, -1 / 6, 1.0):
@@ -107,72 +109,99 @@
     return 2.0 * s * s - 1.0, -2.0 * s * c
 
 
-def pairs(x):
-    lane = lax.broadcasted_iota(jnp.int32, (16, 128), 1)
-    u, v = x[:16], x[16:]
-    ur = pltpu.roll(u, 64, 1)
-    vr = pltpu.roll(v, 64, 1)
-    return jnp.where(lane < 64, u, vr), jnp.where(lane < 64, ur, v)
-
-
-def put(val, a, values):
-    for q, v in enumerate(values):
+def iota(shape, axis):
+    return lax.broadcasted_iota(jnp.int32, shape, axis)
+
+
+def onehot(index, lanes):
+    value = jnp.broadcast_to(index, (lanes, 128)).astype(BF16)
+    hit = value == iota((lanes, 128), 0).astype(F32).astype(BF16)
+    return jnp.where(hit, jnp.ones_like(value), jnp.zeros_like(value))
+
+
+def nt(a, b):
+    return lax.dot_general(a, b, (((1,), (1,)), ((), ())), preferred_element_type=F32)
+
+
+def sort_group(group, band_ref, from_row, from_lane):
+    before = iota((128, 256), 0)
+    lane2 = iota((128, 256), 1)
+    upper = jnp.where((lane2 >= 128) | (before < lane2), 1.0, 0.0).astype(BF16)
+    bi = iota((128, 128), 0)
+    bj = iota((128, 128), 1)
+    lower = jnp.where((bi // 8 == bj // 8) & (bj < bi), 1.0, 0.0).astype(BF16)
+    r16 = iota((16, 128), 0)
+    lane16 = iota((16, 128), 1)
+    rows = (r16 % 8).astype(F32).astype(BF16)
+    for part in range(GROUP):
+        det = group * GROUP + part
+        band = band_ref[det]
+        hits = [jnp.where(band == b, 1.0, 0.0) for b in range(16)]
+        counts = mm(jnp.concatenate(hits, axis=0).astype(BF16), upper)
+        total = counts[:, :128] + mm(lower, counts[:, 128:].astype(BF16))
+        rank = jnp.zeros((8, 128), F32)
+        for b in range(16):
+            rank = rank + hits[b] * total[8 * b : 8 * b + 8]
+        place = jnp.where(band >= 8, rank + 64.0, rank)
+        row = (band % 8).astype(F32)
+        left = []
+        right = []
+        for i in range(8):
+            here = jnp.broadcast_to(row[i : i + 1], (16, 128)).astype(BF16) == rows
+            digit = jnp.where(r16 < 8, i, lane16).astype(F32).astype(BF16)
+            left.append(jnp.where(here, digit, jnp.zeros_like(digit)))
+            right.append(onehot(place[i : i + 1], 128))
+        source = nt(jnp.concatenate(left, axis=1), jnp.concatenate(right, axis=1))
+        from_row[det] = source[:8].astype(jnp.int32)
+        from_lane[det] = source[8:].astype(jnp.int32)
+
+
+def pick(value, det, from_row, from_lane):
+    row = from_row[det]
+    lane = from_lane[det]
+    out = jnp.zeros((8, 128), F32)
+    for i in range(8):
+        line = jnp.broadcast_to(value[det, i : i + 1, :], (8, 128))
+        out = jnp.where(row == i, jnp.take_along_axis(line, lane, axis=1, mode="promise_in_bounds"), out)
+    return out
+
+
+def to_bands(values, outs, from_row, from_lane):
+    lane = iota((8, 128), 1)
+    for p in range(16):
+        for value, out in zip(values, outs):
+            u = pick(value, 2 * p, from_row, from_lane)
+            v = pick(value, 2 * p + 1, from_row, from_lane)
+            out[0:8, p, :] = jnp.where(lane < 64, u, pltpu.roll(v, 64, 1))
+            out[8:16, p, :] = jnp.where(lane < 64, pltpu.roll(u, 64, 1), v)
+
+
+def parts_of(values):
+    parts = []
+    for v in values:
         hi = v.astype(BF16).astype(F32)
-        for k, part in enumerate((hi, v - hi)):
-            val[2 * q + k, 2 * a], val[2 * q + k, 2 * a + 1] = pairs(part)
-
-
-def tile_sum(j, count, val, mi, lt, rt, term):
-    im = lax.broadcasted_iota(jnp.int32, (64, 128), 0).astype(F32).astype(BF16)
+        parts += [hi, v - hi]
+    return parts
+
+
+def map_lines(parts, cell_row):
+    rows = iota((16, 128), 0).astype(F32).astype(BF16)
+    left = []
     for k in range(16):
-        mask = jnp.broadcast_to(mi[j, k : k + 1, :], (64, 128)).astype(BF16) == im
-        for q in range(2 * count):
-            vb = jnp.broadcast_to(val[q, j, k : k + 1, :], (64, 128)).astype(BF16)
-            lt[k, 64 * q : 64 * q + 64, :] = jnp.where(mask, vb, jnp.zeros_like(vb))
-    left = jnp.concatenate([lt[k] for k in range(16)], axis=1)
-    right = jnp.concatenate([rt[j, k] for k in range(16)], axis=1)
-    acc = lax.dot_general(
-        left, right, (((1,), (1,)), ((), ())), preferred_element_type=F32
-    ).reshape(count, 2, 64, 256)
-    term[j] = acc[:, 0] + acc[:, 1]
-
-
-def columns(j, ni, rt):
-    it = lax.broadcasted_iota(jnp.int32, (256, 128), 0).astype(F32).astype(BF16)
-    for k in range(16):
-        nb = jnp.broadcast_to(ni[j, k : k + 1, :], (256, 128)).astype(BF16)
-        rt[j, k] = jnp.where(nb == it, jnp.ones_like(nb), jnp.zeros_like(nb))
-
-
-def by_slot(slots, term, count, maps):
-    marks = [slots[j].astype(F32) for j in range(16)]
-    for h in range(2):
-
-        def one(q, carry):
-            every = jnp.zeros((64, 128), F32)
-            second = jnp.zeros((64, 128), F32)
-            for j in range(16):
-                t = term[j, q, :, 128 * h : 128 * h + 128]
-                every = every + t
-                second = second + t * marks[j]
-            first = every - second
-            for b in range(8):
-                maps[8 * h + b, 0, q] = first[8 * b : 8 * b + 8]
-                maps[8 * h + b, 1, q] = second[8 * b : 8 * b + 8]
-            return carry
-
-        lax.fori_loop(0, count, one, 0)
-
-
-def spread(sub0, sub1, count, got, out):
-    for q in range(count):
-        a0 = got[0, 0, q]
-        a1 = got[0, 1, q]
-        for i in range(1, ND):
-            a0 = a0 + got[i, 0, q]
-            a1 = a1 + got[i, 1, q]
-        for n in range(NT):
-            out[n, q] = jnp.where(sub0 == n, a0, 0.0) + jnp.where(sub1 == n, a1, 0.0)
+        here = jnp.broadcast_to(cell_row[k : k + 1], (16, 128)).astype(BF16) == rows
+        lines = []
+        for part in parts:
+            line = jnp.broadcast_to(part[k : k + 1], (16, 128)).astype(BF16)
+            lines.append(jnp.where(here, line, jnp.zeros_like(line)))
+        left.append(jnp.concatenate(lines, axis=0))
+    return left
+
+
+def spread(sub0, sub1, count, acc, out):
+    both = acc[...].reshape(count, 2, 16, 128)
+    both = both[:, 0] + both[:, 1]
+    for n in range(NT):
+        out[n] = jnp.where(sub0 == n, both[:, :8], 0.0) + jnp.where(sub1 == n, both[:, 8:], 0.0)
 
 
 def noise_filtering(x, g, ah, al, bh, bl, ch, cl, ih, il, turn):
@@ -197,23 +226,19 @@
 def fused_kernel(
     slots,
     sub,
-    tod,
-    gain,
-    weight,
-    couple,
-    w_ref,
-    row_ref,
-    col_ref,
-    ang_ref,
-    ah,
-    al,
-    ih,
-    il,
-    bh,
-    bl,
-    ch,
-    cl,
-    turn,
+    *refs,
+):
+    far, refs = refs[:17], refs[17:]
+    out, near, load_sem, refs = refs[0], refs[1:18], refs[18], refs[19:]
+    fused_body(slots, sub, far, near, load_sem, out, *refs)
+
+
+def fused_body(
+    slots,
+    sub,
+    far,
+    near,
+    load_sem,
     out,
     ybuf,
     yin,
@@ -226,20 +251,21 @@
     ftmp,
     obuf,
     cin,
+    wt,
+    bandt,
+    cellt,
+    angt,
+    cleant,
+    from_row,
+    from_lane,
+    early,
+    earlyin,
+    late,
+    latein,
     wcs,
-    valc,
-    vals,
-    mi,
-    ni,
-    ltc,
-    lts,
     rt,
-    termc,
-    terms,
-    mapc,
-    maps,
-    rsc,
-    rss,
+    accc,
+    accs,
     tbc,
     tbs,
     ubc,
@@ -249,45 +275,53 @@
     sz,
     sf,
     so,
-    sc,
-    ss,
+    se,
+    sl,
     tc_sem,
     ts_sem,
 ):
     me_d = lax.axis_index("det")
     me_t = lax.axis_index("tm")
+    loads = []
+    for i in range(17):
+        load = pltpu.make_async_copy(far[i], near[i], load_sem.at[i])
+        load.start()
+        loads.append(load)
     barrier = greet(me_d, me_t)
+    (tod, weight, w_ref, row_ref, col_ref, ang_ref, gain, couple) = near[:8]
+    (ah, al, ih, il, bh, bl, ch, cl, turn) = near[8:]
+    loads[0].wait()
+    loads[1].wait()
     wsp = split(weight[...])
     for a in range(8):
         x = tod[:, 128 * a : 128 * a + 128]
         ybuf[:, a, :] = dot3(wsp, split(x))
         sbuf[:, a, :] = x
+    for load in loads[2:6]:
+        load.wait()
+    half = iota((32, 128), 1) < 64
+    for a in range(8):
+        sl_a = slice(128 * a, 128 * a + 128)
+        row = row_ref[:, sl_a]
+        slot = jnp.where(half, slots[2 * a], slots[2 * a + 1])
+        wt[:, a, :] = w_ref[:, sl_a]
+        angt[:, a, :] = ang_ref[:, sl_a].astype(F32)
+        bandt[:, a, :] = row // 8
+        cellt[:, a, :] = ((slot * 8 + row % 8) * 128 + col_ref[:, sl_a]).astype(F32)
+
+    def sort(group, carry):
+        sort_group(group, bandt, from_row, from_lane)
+        return carry
+
+    lax.fori_loop(CUTS[0], CUTS[1], sort, 0)
     pl.semaphore_wait(barrier, ND - 1 + NT - 1)
     copies = send("det", ND, me_d, lambda p: ybuf.at[pl.ds(2 * p, 2)], yin, sy)
     copies += send("tm", NT, me_t, lambda p: sbuf.at[pl.ds(4 * p, 4)], xin, sx)
     yin[me_d] = ybuf[pl.ds(2 * me_d, 2)]
     xin[me_t] = sbuf[pl.ds(4 * me_t, 4)]
-    g = gain[...]
-    gfull = jnp.concatenate([g[:, :64].T, g[:, 64:].T], axis=1)
-    for a in range(8):
-        sl = slice(128 * a, 128 * a + 128)
-        w = w_ref[:, sl]
-        c, s = trig(ang_ref[:, sl])
-        wc = w * c
-        ws = w * s
-        wcs[0, a] = wc
-        wcs[1, a] = ws
-        put(valc, a, (w, wc, ws, wc * c, wc * s))
-        row = row_ref[:, sl]
-        mi[2 * a], mi[2 * a + 1] = pairs((row % 64).astype(F32))
-        ni[2 * a], ni[2 * a + 1] = pairs((row // 64 * 128 + col_ref[:, sl]).astype(F32))
-
-    def cov_tile(j, carry):
-        columns(j, ni, rt)
-        tile_sum(j, 5, valc, mi, ltc, rt, termc)
-        return carry
-
-    lax.fori_loop(CUTS[0], CUTS[1], cov_tile, 0)
+    accc[...] = jnp.zeros_like(accc)
+    accs[...] = jnp.zeros_like(accs)
+    lax.fori_loop(CUTS[1], CUTS[2], sort, 0)
     arrive("det", ND, me_d, yin, sy)
     z = yin[0]
     for i in range(1, ND):
@@ -295,7 +329,18 @@
     zbuf[...] = z
     copies += send("tm", NT, me_t, lambda p: zbuf, zin, sz)
     zin[me_t] = z
-    lax.fori_loop(CUTS[1], CUTS[2], cov_tile, 0)
+    to_bands(
+        (wt, cellt, angt),
+        [early.at[:, i] for i in range(3)],
+        from_row,
+        from_lane,
+    )
+    copies += send("det", ND, me_d, lambda p: early.at[p], earlyin, se)
+    earlyin[me_d] = early[me_d]
+    for load in loads[6:]:
+        load.wait()
+    g = gain[...]
+    gfull = jnp.concatenate([g[:, :64].T, g[:, 64:].T], axis=1)
     arrive("tm", NT, me_t, xin, sx)
     arrive("tm", NT, me_t, zin, sz)
     cols = [jnp.concatenate([xin[m, e] for m in range(NT)], axis=0) for e in range(4)]
@@ -314,37 +359,67 @@
     copies += send("tm", NT, me_t, lambda p: obuf.at[p], cin, so)
     fin[me_d] = mine
     cin[me_t] = obuf[me_t]
-    lax.fori_loop(CUTS[2], CUTS[3], cov_tile, 0)
-    by_slot(slots, termc, 5, mapc)
-    copies += send("det", ND, me_d, lambda p: mapc.at[p], rsc, sc)
-    rsc[me_d] = mapc[me_d]
+    arrive("det", ND, me_d, earlyin, se)
+
+    def cov_step(step, carry):
+        left = []
+        right = []
+        for i in range(2):
+            d = 2 * step + i
+            w = earlyin[d, 0]
+            cell = earlyin[d, 1].astype(jnp.int32)
+            c, s = trig(earlyin[d, 2])
+            wc = w * c
+            ws = w * s
+            cell_row = (cell // 128).astype(F32)
+            wcs[d, 0] = wc
+            wcs[d, 1] = ws
+            wcs[d, 2] = cell_row
+            column = (cell % 128).astype(F32)
+            for k in range(16):
+                hit = onehot(column[k : k + 1], 128)
+                rt[d, k] = hit
+                right.append(hit)
+            left += map_lines(parts_of((w, wc, ws, wc * c, wc * s)), cell_row)
+        accc[...] += nt(jnp.concatenate(left, axis=1), jnp.concatenate(right, axis=1))
+        return carry
+
+    lax.fori_loop(STEPS[0], STEPS[1], cov_step, 0)
     arrive("det", ND, me_d, fin, sf)
     arrive("tm", NT, me_t, cin, so)
     csp = split(couple[...])
     for a in range(8):
         modes = fin[:, :, a, :].reshape(32, 128)
-        clean = cin[:, :, a, :].reshape(32, 128) - dot3(csp, split(modes))
-        w = w_ref[:, 128 * a : 128 * a + 128]
-        put(vals, a, (w * clean, wcs[0, a] * clean, wcs[1, a] * clean))
-
-    def signal_tile(j, carry):
-        tile_sum(j, 3, vals, mi, lts, rt, terms)
-        return carry
-
-    lax.fori_loop(0, 16, signal_tile, 0)
-    by_slot(slots, terms, 3, maps)
-    copies += send("det", ND, me_d, lambda p: maps.at[p], rss, ss)
-    rss[me_d] = maps[me_d]
-    sub0 = sub[me_t, 0]
-    sub1 = sub[me_t, 1]
-    arrive("det", ND, me_d, rsc, sc)
-    spread(sub0, sub1, 5, rsc, tbc)
+        cleant[:, a, :] = cin[:, :, a, :].reshape(32, 128) - dot3(csp, split(modes))
+    to_bands((cleant,), (late,), from_row, from_lane)
+    copies += send("det", ND, me_d, lambda p: late.at[p], latein, sl)
+    latein[me_d] = late[me_d]
+    sub0 = sub[0, me_t]
+    sub1 = sub[1, me_t]
+    lax.fori_loop(STEPS[1], STEPS[2], cov_step, 0)
+    spread(sub0, sub1, 5, accc, tbc)
     copies += send("tm", NT, me_t, lambda p: tbc.at[p], ubc, tc_sem)
     ubc[me_t] = tbc[me_t]
-    arrive("det", ND, me_d, rss, ss)
-    spread(sub0, sub1, 3, rss, tbs)
-    copies += send("tm", NT, me_t, lambda p: tbs.at[p], ubs, ts_sem)
+    arrive("det", ND, me_d, latein, sl)
+
+    def signal_step(step, carry):
+        left = []
+        right = []
+        for i in range(4):
+            d = 4 * step + i
+            x = latein[d]
+            values = (earlyin[d, 0] * x, wcs[d, 0] * x, wcs[d, 1] * x)
+            left += map_lines(parts_of(values), wcs[d, 2])
+            right += [rt[d, k] for k in range(16)]
+        accs[...] += nt(jnp.concatenate(left, axis=1), jnp.concatenate(right, axis=1))
+        return carry
+
+    lax.fori_loop(0, ND // 4, signal_step, 0)
+    spread(sub0, sub1, 3, accs, tbs)
+    final = send("tm", NT, me_t, lambda p: tbs.at[p], ubs, ts_sem)
     ubs[me_t] = tbs[me_t]
+    for c in copies:
+        c.wait_send()
     arrive("tm", NT, me_t, ubc, tc_sem)
     total = ubc[0]
     for i in range(1, NT):
@@ -355,7 +430,7 @@
     for i in range(1, NT):
         total = total + ubs[i]
     out[5:] = total
-    for c in copies:
+    for c in final:
         c.wait_send()
 
 
@@ -396,12 +471,25 @@
     def sems(size):
         return pltpu.SemaphoreType.DMA((2, size))
 
+    operands = (
+        tod,
+        mode_weight,
+        sample_weight,
+        pix_row,
+        pix_col,
+        angle_bin,
+        noise_filter.reshape(64, 128),
+        mode_coupling,
+        *tables,
+    )
     tot = pl.pallas_call(
         fused_kernel,
         out_shape=jax.ShapeDtypeStruct((8, 8, 128), F32),
-        in_specs=[sm, sm] + [vm] * 17,
+        in_specs=[sm, sm] + [pl.BlockSpec(memory_space=pl.ANY)] * 17,
         out_specs=vm,
-        scratch_shapes=[
+        scratch_shapes=[vmem(*o.shape, dtype=o.dtype) for o in operands]
+        + [
+            pltpu.SemaphoreType.DMA((17,)),
             vmem(32, 8, 128),
             vmem(ND, 2, 8, 128),
             vmem(32, 8, 128),
@@ -413,20 +501,21 @@
             vmem(NT, 2, 8, 128),
             vmem(NT, 4, 8, 128),
             vmem(NT, 4, 8, 128),
-            vmem(2, 8, 32, 128),
-            vmem(10, 16, 16, 128),
-            vmem(6, 16, 16, 128),
-            vmem(16, 16, 128),
-            vmem(16, 16, 128),
-            vmem(16, 640, 128, dtype=BF16),
-            vmem(16, 384, 128, dtype=BF16),
-            vmem(16, 16, 256, 128, dtype=BF16),
-            vmem(16, 5, 64, 256),
-            vmem(16, 3, 64, 256),
-            vmem(ND, 2, 5, 8, 128),
-            vmem(ND, 2, 3, 8, 128),
-            vmem(ND, 2, 5, 8, 128),
-            vmem(ND, 2, 3, 8, 128),
+            vmem(32, 8, 128),
+            vmem(32, 8, 128, dtype=jnp.int32),
+            vmem(32, 8, 128),
+            vmem(32, 8, 128),
+            vmem(32, 8, 128),
+            vmem(32, 8, 128, dtype=jnp.int32),
+            vmem(32, 8, 128, dtype=jnp.int32),
+            vmem(ND, 3, 16, 128),
+            vmem(ND, 3, 16, 128),
+            vmem(ND, 16, 128),
+            vmem(ND, 16, 128),
+            vmem(ND, 3, 16, 128),
+            vmem(ND, 16, 128, 128, dtype=BF16),
+            vmem(160, 128),
+            vmem(96, 128),
             vmem(NT, 5, 8, 128),
             vmem(NT, 3, 8, 128),
             vmem(NT, 5, 8, 128),
@@ -444,19 +533,7 @@
         compiler_params=pltpu.CompilerParams(
             collective_id=0, has_side_effects=True, vmem_limit_bytes=56 << 20
         ),
-    )(
-        tile_slot,
-        slot_submap,
-        tod,
-        noise_filter.reshape(64, 128),
-        mode_weight,
-        mode_coupling,
-        sample_weight,
-        pix_row,
-        pix_col,
-        angle_bin,
-        *tables,
-    )
+    )(tile_slot, slot_submap.T, *operands)
     return pl.pallas_call(
         finish_kernel,
         out_shape=(

time: 56.3 us -> 48.5 us (0.86)
  Pallas kernels: 54.1 us -> 47.7 us
  local copies, waits for them, and re-layouts: 1.34 us -> 0 us
    pallas_call x1, Pallas kernels: 52.7 us -> 46.3 us  [body(): pl.pallas_call(fused_kernel, out_shape=jax.ShapeDtypeStruct((8, 8, 128),...]
    unnamed x3 -> x0, local copies, waits for them, and re-layouts: 1.34 us -> none
where the time goes in v3:
time: 48.5 us; the launch traced here: 48.3 us
  Pallas kernels  47.7 us (98%)
  between operations  0.64 us (1%)
    pallas_call x1, Pallas kernels, body(): pl.pallas_call(fused_kernel, out_shape=jax.ShapeDtypeStruct((8, 8, 128),...  46.3 us
    pallas_call x1, Pallas kernels, body(): pl.pallas_call(finish_kernel, out_shape=(jax.ShapeDtypeStruct((1, 3, 8, 1...  1.38 us

profile of v3, /device:TPU:1, one launch (start us, length us, event | category | flops | bytes accessed | tf_op | source)
XLA Modules:
  0.0 48.3 jit_solution(248695187241271092)
XLA Ops:
  0.6 46.3 %shard_map.194.tot = f32[8,8,128]{2,1,0:T(8,128)} custom-call(s32[16]{0:T(128)} %slots.1, s32[2,8]{1,0:T(2,128)} %bitcast.3, f32[32,1024]{1,0:T(8,128)} %refs_0_.1, f32[32,32]{1,0:T(8,128)} %refs_1_.1, f32[32,1024]{1,0:T(8,128)} %refs_2_.1, s32[32,1024]{1,0:T(8,128)} %refs_3_.1, s32[32,1024]{1,0:T(8,128)} %refs_4_.1, s32[32,1024]{1,0:T(8,128)} %refs_5_.1, ...), custom_call_target="tpu_custom_call" | custom-call | tf_op jit(solution)/shard_map/pallas_call | solution.py:485
  46.9 1.4 %shard_map.195 = (f32[1,3,8,128]{3,2,1,0:T(8,128)}, f32[1,3,3,8,128]{4,3,2,1,0:T(8,128)}) custom-call(f32[8,8,128]{2,1,0:T(8,128)} %shard_map.194.tot), custom_call_target="tpu_custom_call" | custom-call | tf_op jit(solution)/shard_map/pallas_call | solution.py:537

commit v4 on v3

--- a/solution.py
+++ b/solution.py
@@ -15,7 +15,7 @@
 NT = 8
 GROUP = 8
 CUTS = (0, 1, 4)
-STEPS = (0, 4, 8)
+STEPS = (0, 6, 8)
 
 
 def split_const(table):
@@ -83,17 +83,20 @@
     return copies
 
 
+def arrive_one(axis, peer, dst_buf, sems):
+    pltpu.make_async_remote_copy(
+        src_ref=dst_buf.at[peer],
+        dst_ref=dst_buf.at[peer],
+        send_sem=sems.at[0, peer],
+        recv_sem=sems.at[1, peer],
+        device_id={axis: peer},
+        device_id_type=MESH,
+    ).wait_recv()
+
+
 def arrive(axis, size, me, dst_buf, sems):
     for i in range(1, size):
-        peer = (me + i) % size
-        pltpu.make_async_remote_copy(
-            src_ref=dst_buf.at[peer],
-            dst_ref=dst_buf.at[peer],
-            send_sem=sems.at[0, peer],
-            recv_sem=sems.at[1, peer],
-            device_id={axis: peer},
-            device_id_type=MESH,
-        ).wait_recv()
+        arrive_one(axis, (me + i) % size, dst_buf, sems)
 
 
 def trig(ang):
@@ -123,37 +126,72 @@
     return lax.dot_general(a, b, (((1,), (1,)), ((), ())), preferred_element_type=F32)
 
 
-def sort_group(group, band_ref, from_row, from_lane):
+def sort_group(group, band_ref, fields, from_row, from_lane, outs):
     before = iota((128, 256), 0)
     lane2 = iota((128, 256), 1)
     upper = jnp.where((lane2 >= 128) | (before < lane2), 1.0, 0.0).astype(BF16)
-    bi = iota((128, 128), 0)
-    bj = iota((128, 128), 1)
-    lower = jnp.where((bi // 8 == bj // 8) & (bj < bi), 1.0, 0.0).astype(BF16)
     r16 = iota((16, 128), 0)
     lane16 = iota((16, 128), 1)
+    lane = iota((8, 128), 1)
     rows = (r16 % 8).astype(F32).astype(BF16)
+    w_ref, cell_ref, col_ref, ang_ref = fields
+    moved = []
+    rank16 = r16.astype(F32).astype(BF16)
+    hits = []
     for part in range(GROUP):
         det = group * GROUP + part
-        band = band_ref[det]
-        hits = [jnp.where(band == b, 1.0, 0.0) for b in range(16)]
-        counts = mm(jnp.concatenate(hits, axis=0).astype(BF16), upper)
-        total = counts[:, :128] + mm(lower, counts[:, 128:].astype(BF16))
-        rank = jnp.zeros((8, 128), F32)
-        for b in range(16):
-            rank = rank + hits[b] * total[8 * b : 8 * b + 8]
-        place = jnp.where(band >= 8, rank + 64.0, rank)
-        row = (band % 8).astype(F32)
+        for i in range(8):
+            band = jnp.broadcast_to(band_ref[det, i : i + 1, :], (16, 128)).astype(BF16)
+            hits.append(jnp.where(band == rank16, jnp.ones_like(band), jnp.zeros_like(band)))
+    counts = mm(jnp.concatenate(hits, axis=0), upper)
+    for part in range(GROUP):
+        det = group * GROUP + part
+        row = band_ref[det] % 8.0
+        offset = jnp.where(r16 >= 8, 64.0, 0.0)
+        places = []
+        for i in range(8):
+            k = 8 * part + i
+            here = counts[16 * k : 16 * k + 16]
+            spot = hits[k].astype(F32) * (here[:, :128] + offset)
+            places.append(jnp.sum(spot, axis=0, keepdims=True))
+            offset = offset + here[:, 128:]
+        w = w_ref[det]
+        w_hi = w.astype(BF16).astype(F32)
+        w_lo = w - w_hi
+        cell = cell_ref[det]
+        col = col_ref[det]
+        ang = ang_ref[det]
         left = []
         right = []
         for i in range(8):
             here = jnp.broadcast_to(row[i : i + 1], (16, 128)).astype(BF16) == rows
             digit = jnp.where(r16 < 8, i, lane16).astype(F32).astype(BF16)
-            left.append(jnp.where(here, digit, jnp.zeros_like(digit)))
-            right.append(onehot(place[i : i + 1], 128))
+            lines = [digit]
+            for u, v in ((w_hi, w_lo), (cell, col), (ang, ang)):
+                u = jnp.broadcast_to(u[i : i + 1], (8, 128))
+                v = jnp.broadcast_to(v[i : i + 1], (8, 128))
+                lines.append(jnp.concatenate([u, v], axis=0).astype(BF16))
+            lines = [jnp.where(here, line, jnp.zeros_like(line)) for line in lines]
+            left.append(jnp.concatenate(lines, axis=0))
+            right.append(onehot(places[i], 128))
         source = nt(jnp.concatenate(left, axis=1), jnp.concatenate(right, axis=1))
         from_row[det] = source[:8].astype(jnp.int32)
-        from_lane[det] = source[8:].astype(jnp.int32)
+        from_lane[det] = source[8:16].astype(jnp.int32)
+        moved.append(
+            (
+                source[16:24] + source[24:32],
+                source[32:40] * 128.0 + source[40:48],
+                source[48:56],
+            )
+        )
+    for k in range(GROUP // 2):
+        p = group * (GROUP // 2) + k
+        for i in range(3):
+            u, v = moved[2 * k][i], moved[2 * k + 1][i]
+            low = jnp.where(lane < 64, u, pltpu.roll(v, 64, 1))
+            high = jnp.where(lane < 64, pltpu.roll(u, 64, 1), v)
+            outs[0:8, i, pl.ds(p, 1), :] = low.reshape(8, 1, 128)
+            outs[8:16, i, pl.ds(p, 1), :] = high.reshape(8, 1, 128)
 
 
 def pick(value, det, from_row, from_lane):
@@ -254,6 +292,7 @@
     wt,
     bandt,
     cellt,
+    colt,
     angt,
     cleant,
     from_row,
@@ -306,11 +345,12 @@
         slot = jnp.where(half, slots[2 * a], slots[2 * a + 1])
         wt[:, a, :] = w_ref[:, sl_a]
         angt[:, a, :] = ang_ref[:, sl_a].astype(F32)
-        bandt[:, a, :] = row // 8
-        cellt[:, a, :] = ((slot * 8 + row % 8) * 128 + col_ref[:, sl_a]).astype(F32)
+        bandt[:, a, :] = (row // 8).astype(F32)
+        cellt[:, a, :] = (slot * 8 + row % 8).astype(F32)
+        colt[:, a, :] = col_ref[:, sl_a].astype(F32)
 
     def sort(group, carry):
-        sort_group(group, bandt, from_row, from_lane)
+        sort_group(group, bandt, (wt, cellt, colt, angt), from_row, from_lane, early)
         return carry
 
     lax.fori_loop(CUTS[0], CUTS[1], sort, 0)
@@ -322,6 +362,8 @@
     accc[...] = jnp.zeros_like(accc)
     accs[...] = jnp.zeros_like(accs)
     lax.fori_loop(CUTS[1], CUTS[2], sort, 0)
+    copies += send("det", ND, me_d, lambda p: early.at[p], earlyin, se)
+    earlyin[me_d] = early[me_d]
     arrive("det", ND, me_d, yin, sy)
     z = yin[0]
     for i in range(1, ND):
@@ -329,14 +371,6 @@
     zbuf[...] = z
     copies += send("tm", NT, me_t, lambda p: zbuf, zin, sz)
     zin[me_t] = z
-    to_bands(
-        (wt, cellt, angt),
-        [early.at[:, i] for i in range(3)],
-        from_row,
-        from_lane,
-    )
-    copies += send("det", ND, me_d, lambda p: early.at[p], earlyin, se)
-    earlyin[me_d] = early[me_d]
     for load in loads[6:]:
         load.wait()
     g = gain[...]
@@ -400,13 +434,20 @@
     spread(sub0, sub1, 5, accc, tbc)
     copies += send("tm", NT, me_t, lambda p: tbc.at[p], ubc, tc_sem)
     ubc[me_t] = tbc[me_t]
-    arrive("det", ND, me_d, latein, sl)
-
     def signal_step(step, carry):
+        dz = step + step // 2 - 2 * (step // 3)
+        row = (me_d // 4 + dz) % 4 * 4
         left = []
         right = []
-        for i in range(4):
-            d = 4 * step + i
+
+        @pl.when(step > 0)
+        def _():
+            arrive_one("det", row + me_d % 4, latein, sl)
+
+        for dx in (1, 3, 2):
+            arrive_one("det", row + (me_d + dx) % 4, latein, sl)
+        for dx in range(4):
+            d = row + (me_d + dx) % 4
             x = latein[d]
             values = (earlyin[d, 0] * x, wcs[d, 0] * x, wcs[d, 1] * x)
             left += map_lines(parts_of(values), wcs[d, 2])
@@ -414,7 +455,7 @@
         accs[...] += nt(jnp.concatenate(left, axis=1), jnp.concatenate(right, axis=1))
         return carry
 
-    lax.fori_loop(0, ND // 4, signal_step, 0)
+    lax.fori_loop(0, 4, signal_step, 0)
     spread(sub0, sub1, 3, accs, tbs)
     final = send("tm", NT, me_t, lambda p: tbs.at[p], ubs, ts_sem)
     ubs[me_t] = tbs[me_t]
@@ -502,7 +543,8 @@
             vmem(NT, 4, 8, 128),
             vmem(NT, 4, 8, 128),
             vmem(32, 8, 128),
-            vmem(32, 8, 128, dtype=jnp.int32),
+            vmem(32, 8, 128),
+            vmem(32, 8, 128),
             vmem(32, 8, 128),
             vmem(32, 8, 128),
             vmem(32, 8, 128),

time: 48.5 us -> 41 us (0.85)
  Pallas kernels: 47.7 us -> 40.2 us
    pallas_call x1, Pallas kernels: 46.3 us -> 38.8 us  [body(): pl.pallas_call(fused_kernel, out_shape=jax.ShapeDtypeStruct((8, 8, 128),...]
where the time goes in v4:
time: 41 us; the launch traced here: 40.8 us
  Pallas kernels  40.2 us (98%)
  between operations  0.64 us (2%)
    pallas_call x1, Pallas kernels, body(): pl.pallas_call(fused_kernel, out_shape=jax.ShapeDtypeStruct((8, 8, 128),...  38.8 us
    pallas_call x1, Pallas kernels, body(): pl.pallas_call(finish_kernel, out_shape=(jax.ShapeDtypeStruct((1, 3, 8, 1...  1.38 us

profile of v4, /device:TPU:1, one launch (start us, length us, event | category | flops | bytes accessed | tf_op | source)
XLA Modules:
  0.0 40.8 jit_solution(12245610177900959721)
XLA Ops:
  0.6 38.8 %shard_map.194.tot = f32[8,8,128]{2,1,0:T(8,128)} custom-call(s32[16]{0:T(128)} %slots.1, s32[2,8]{1,0:T(2,128)} %bitcast.3, f32[32,1024]{1,0:T(8,128)} %refs_0_.1, f32[32,32]{1,0:T(8,128)} %refs_1_.1, f32[32,1024]{1,0:T(8,128)} %refs_2_.1, s32[32,1024]{1,0:T(8,128)} %refs_3_.1, s32[32,1024]{1,0:T(8,128)} %refs_4_.1, s32[32,1024]{1,0:T(8,128)} %refs_5_.1, ...), custom_call_target="tpu_custom_call" | custom-call | tf_op jit(solution)/shard_map/pallas_call | solution.py:526
  39.4 1.4 %shard_map.195 = (f32[1,3,8,128]{3,2,1,0:T(8,128)}, f32[1,3,3,8,128]{4,3,2,1,0:T(8,128)}) custom-call(f32[8,8,128]{2,1,0:T(8,128)} %shard_map.194.tot), custom_call_target="tpu_custom_call" | custom-call | tf_op jit(solution)/shard_map/pallas_call | solution.py:579

commit v5 on v4

--- a/solution.py
+++ b/solution.py
@@ -53,23 +53,27 @@
     return mm(a[0], b[0]) + (mm(a[0], b[1]) + mm(a[1], b[0]))
 
 
+def peers(axis, me):
+    if axis == "tm":
+        return [(me + i) % NT for i in (4, 5, 3, 2, 6, 7, 1)]
+    steps = ((dz, dx) for dz in range(4) for dx in range(4) if dz or dx)
+    steps = sorted(steps, key=lambda o: -(min(o[0], 4 - o[0]) + min(o[1], 4 - o[1])))
+    return [(me // 4 + dz) % 4 * 4 + (me + dx) % 4 for dz, dx in steps]
+
+
 def greet(me_d, me_t):
     barrier = pltpu.get_barrier_semaphore()
-    for i in range(1, ND):
-        pl.semaphore_signal(
-            barrier, inc=1, device_id={"det": (me_d + i) % ND}, device_id_type=MESH
-        )
-    for i in range(1, NT):
-        pl.semaphore_signal(
-            barrier, inc=1, device_id={"tm": (me_t + i) % NT}, device_id_type=MESH
-        )
+    for axis, me in (("det", me_d), ("tm", me_t)):
+        for peer in peers(axis, me):
+            pl.semaphore_signal(
+                barrier, inc=1, device_id={axis: peer}, device_id_type=MESH
+            )
     return barrier
 
 
 def send(axis, size, me, src_of, dst_buf, sems):
     copies = []
-    for i in range(1, size):
-        peer = (me + i) % size
+    for peer in peers(axis, me):
         copy = pltpu.make_async_remote_copy(
             src_ref=src_of(peer),
             dst_ref=dst_buf.at[me],
@@ -321,12 +325,12 @@
 ):
     me_d = lax.axis_index("det")
     me_t = lax.axis_index("tm")
+    barrier = greet(me_d, me_t)
     loads = []
     for i in range(17):
         load = pltpu.make_async_copy(far[i], near[i], load_sem.at[i])
         load.start()
         loads.append(load)
-    barrier = greet(me_d, me_t)
     (tod, weight, w_ref, row_ref, col_ref, ang_ref, gain, couple) = near[:8]
     (ah, al, ih, il, bh, bl, ch, cl, turn) = near[8:]
     loads[0].wait()
@@ -376,23 +380,24 @@
     g = gain[...]
     gfull = jnp.concatenate([g[:, :64].T, g[:, 64:].T], axis=1)
     arrive("tm", NT, me_t, xin, sx)
-    arrive("tm", NT, me_t, zin, sz)
+    filt = (gfull, ah, al, bh, bl, ch, cl, ih, il, turn)
     cols = [jnp.concatenate([xin[m, e] for m in range(NT)], axis=0) for e in range(4)]
-    cols += [jnp.concatenate([zin[m, e] for m in range(NT)], axis=0) for e in range(2)]
-    f = noise_filtering(
-        jnp.concatenate(cols, axis=1), gfull, ah, al, bh, bl, ch, cl, ih, il, turn
-    )
+    f = noise_filtering(jnp.concatenate(cols, axis=1), *filt)
     for m in range(NT):
         for e in range(4):
             obuf[m, e] = f[8 * m : 8 * m + 8, 128 * e : 128 * e + 128]
+    copies += send("tm", NT, me_t, lambda p: obuf.at[p], cin, so)
+    cin[me_t] = obuf[me_t]
+    arrive("tm", NT, me_t, zin, sz)
+    cols = [jnp.concatenate([zin[m, e] for m in range(NT)], axis=0) for e in range(2)]
+    f = noise_filtering(jnp.concatenate(cols, axis=1), *filt)
+    for m in range(NT):
         for e in range(2):
-            ftmp[m, e] = f[8 * m : 8 * m + 8, 512 + 128 * e : 640 + 128 * e]
+            ftmp[m, e] = f[8 * m : 8 * m + 8, 128 * e : 128 * e + 128]
     mine = ftmp[me_t]
     fbuf[...] = mine
     copies += send("det", ND, me_d, lambda p: fbuf, fin, sf)
-    copies += send("tm", NT, me_t, lambda p: obuf.at[p], cin, so)
     fin[me_d] = mine
-    cin[me_t] = obuf[me_t]
     arrive("det", ND, me_d, earlyin, se)
 
     def cov_step(step, carry):
@@ -525,7 +530,7 @@
     )
     tot = pl.pallas_call(
         fused_kernel,
-        out_shape=jax.ShapeDtypeStruct((8, 8, 128), F32),
+        out_shape=pltpu.VMEM((8, 8, 128), F32),
         in_specs=[sm, sm] + [pl.BlockSpec(memory_space=pl.ANY)] * 17,
         out_specs=vm,
         scratch_shapes=[vmem(*o.shape, dtype=o.dtype) for o in operands]
@@ -584,7 +589,7 @@
         ),
         in_specs=[vm],
         out_specs=(vm, vm),
-    )(tot)
+    )(pltpu.with_memory_space_constraint(tot, pltpu.VMEM))
 
 
 def solution(mesh):

time: 41 us -> 38.4 us (0.937)
  Pallas kernels: 40.2 us -> 37.6 us
    pallas_call x1, Pallas kernels: 38.8 us -> 37 us  [body(): pl.pallas_call(fused_kernel, out_shape=pltpu.VMEM((8, 8, 128), F32), in_s...]
    pallas_call x1, Pallas kernels: 1.38 us -> 0.62 us  [body(): pl.pallas_call(finish_kernel, out_shape=(jax.ShapeDtypeStruct((1, 3, 8, 1...]
where the time goes in v5:
time: 38.4 us; the launch traced here: 38.3 us
  Pallas kernels  37.6 us (98%)
  between operations  0.64 us (2%)
    pallas_call x1, Pallas kernels, body(): pl.pallas_call(fused_kernel, out_shape=pltpu.VMEM((8, 8, 128), F32), in_s...  37 us

profile of v5, /device:TPU:1, one launch (start us, length us, event | category | flops | bytes accessed | tf_op | source)
XLA Modules:
  0.0 38.3 jit_solution(2503229960100973171)
XLA Ops:
  0.6 37.0 %shard_map.194.tot = f32[8,8,128]{2,1,0:T(8,128)S(1)} custom-call(s32[16]{0:T(128)} %slots.1, s32[2,8]{1,0:T(2,128)} %bitcast.3, f32[32,1024]{1,0:T(8,128)} %refs_0_.1, f32[32,32]{1,0:T(8,128)} %refs_1_.1, f32[32,1024]{1,0:T(8,128)} %refs_2_.1, s32[32,1024]{1,0:T(8,128)} %refs_3_.1, s32[32,1024]{1,0:T(8,128)} %refs_4_.1, s32[32,1024]{1,0:T(8,128)} %refs_5_.1, ...), custom_call_target="tpu_custom_call" | custom-call | tf_op jit(solution)/shard_map/pallas_call | solution.py:531
  37.7 0.6 %shard_map.195 = (f32[1,3,8,128]{3,2,1,0:T(8,128)}, f32[1,3,3,8,128]{4,3,2,1,0:T(8,128)}) custom-call(f32[8,8,128]{2,1,0:T(8,128)S(1)} %shard_map.194.tot), custom_call_target="tpu_custom_call" | custom-call | tf_op jit(solution)/shard_map/pallas_call | solution.py:584
